TPU v7x, 512 devices: a whole 4x8x8 slice. The times are simulated.
512 devices in a mesh: row: 16 (over z_hi, y), col: 32 (over x, z_lo, core).
Axes of the slice: x: 4, y: 8, z: 8 (z_hi: 2, z_lo: 4; z = z_hi * 4 + z_lo), core: 2. Of those that a mesh axis runs over, the one named last changes fastest.
Arguments:
- psi: bfloat16 [131072, 8192], P(('row', 'col')), may hold values from -0.0625 to 0.0625
- hpsi: bfloat16 [131072, 128], P(('row', 'col')), may hold values from -0.796875 to 0.796875
- slab_counts: int32 [512], P(('row', 'col')), may hold values from 1 to 256, 98304 in all
- matrix: float32 [16, 512, 32, 256], P('row', None, 'col'), as said below
Outputs:
- reduced: float32 [16, 512, 32, 256], P('row', None, 'col')
Inputs may be any that keep to these rules, and one draw needn't show every extreme that they name: Slab k's live plane waves are its first slab_counts[k] slots; the rest are padding; the counts sum to 3 * 256 * 512 // 4. The stored matrix is symmetric.
All inputs are finite; a program needn't handle non-finite values.
Results may differ from a plain program's by a relative error of at most 0.0003.
Values sent between devices are 32-bit elements; how exact they have to be, the bound alone decides.
A program may use at most 64 MiB of HBM per device.

v0:
```python
import jax
import jax.numpy as jnp
from jax import lax
from jax.sharding import PartitionSpec as P

TILE = 16


HIGH = lax.Precision.HIGHEST


def filled_up(lines, devices):
    spare = -len(lines) % devices
    return jnp.pad(lines, [(0, spare)] + [(0, 0)] * (lines.ndim - 1))


def laid_out(blocks, dim):
    blocks = jnp.moveaxis(blocks, 0, dim)
    lengths = blocks.shape
    return blocks.reshape(*lengths[:dim], lengths[dim] * lengths[dim + 1], *lengths[dim + 2 :])


def sent_to_all(array, axis):
    devices = lax.axis_size(axis)
    return lax.all_to_all(
        jnp.broadcast_to(array[None], (devices, *array.shape)), axis, 0, 0, tiled=True
    )


def gather_directly(array, axis, dim):
    return laid_out(sent_to_all(array, axis), dim)


def split_up(array, dim, devices):
    before, after = (array.shape[:dim], array.shape[dim + 1 :])
    return jnp.moveaxis(array.reshape(*before, devices, -1, *after), dim, 0)


def summed_on_arrival(array, axis, dim):
    blocks = split_up(array, dim, lax.axis_size(axis))
    arrived = lax.all_to_all(blocks, axis, split_axis=0, concat_axis=0, tiled=True)
    return arrived.sum(axis=0)


def sum_by_parts(array, axes):
    padded = filled_up(array, lax.axis_size(axes))
    whole = gather_directly(summed_on_arrival(padded, axes, 0), axes, 0)
    return lax.slice_in_dim(whole, 0, len(array)).reshape(array.shape)


def together(arrays, axis):
    flat, at, gathered = (jnp.concatenate([a.reshape(-1) for a in arrays]), 0, [])
    subtotal = sum_by_parts(flat, axis)
    for a in arrays:
        gathered.append(subtotal[at : at + a.size].reshape(a.shape))
        at += a.size
    return tuple(gathered)


def sum_by_parts_2(array, axes):
    lines = array.reshape(-1, array.shape[-1])
    padded = filled_up(lines, lax.axis_size(axes))
    whole = gather_directly(summed_on_arrival(padded, axes, 0), axes, 0)
    return lax.slice_in_dim(whole, 0, len(lines)).reshape(array.shape)


def over_copies(array, axis):
    return sent_to_all(array, axis).sum(axis=0)


def lower_solve(factor, rhs):
    return lax.linalg.triangular_solve(factor, rhs, left_side=True, lower=True)


def invert_shifted(shifted):
    normal = jnp.dot(shifted.T, shifted, precision=HIGH)
    factor = jnp.linalg.cholesky(normal)
    first = lower_solve(factor, shifted.T)
    return lax.linalg.triangular_solve(factor, first, left_side=True, lower=True, transpose_a=True)


def per_device(psi, hpsi, slab_counts, matrix):
    prow_id = lax.axis_index("row")
    pcol_id = lax.axis_index("col")
    n_row = lax.axis_size("row")
    n_col = lax.axis_size("col")
    slots = psi.shape[0]
    panel = hpsi.shape[1]
    local_rows = matrix.shape[1]
    local_cols = matrix.shape[3]
    tiles_r = local_rows // TILE
    tiles_c = local_cols // TILE
    valid = jnp.arange(slots, dtype=jnp.int32) < slab_counts[0]
    hcols = jnp.where(valid[:, None], hpsi, jnp.zeros_like(hpsi))
    local_r = jnp.arange(local_rows, dtype=jnp.int32)
    local_c = jnp.arange(local_cols, dtype=jnp.int32)
    row_global = (local_r // TILE * n_row + prow_id) * TILE + local_r % TILE
    col_global = (local_c // TILE * n_col + pcol_id) * TILE + local_c % TILE
    partial_value = lax.dot_general(
        psi, hcols, (((0,), (0,)), ((), ())), preferred_element_type=jnp.float32
    )
    whole = lax.psum(partial_value, ("row", "col"))
    prow = lax.dynamic_index_in_dim(
        whole.reshape(tiles_r, n_row, TILE, panel), prow_id, 1, keepdims=False
    ).reshape(local_rows, panel)
    scols = lax.dynamic_index_in_dim(
        whole.reshape(tiles_c, n_col, TILE, panel), pcol_id, 1, keepdims=False
    ).reshape(local_cols, panel)
    span = jnp.arange(panel, dtype=jnp.int32)
    lower_r = jnp.where((row_global >= panel)[:, None], prow, jnp.zeros_like(prow))
    lower_c = jnp.where((col_global >= panel)[:, None], scols, jnp.zeros_like(scols))
    top_select = (row_global[None, :] == panel + span[:, None]).astype(jnp.float32)
    gram_part = jnp.dot(lower_r.T, lower_r, precision=HIGH)
    top_part = jnp.dot(top_select, prow, precision=HIGH)
    gram, top_rows = together((gram_part, top_part), "row")
    factor = jnp.linalg.cholesky(gram)
    basis_r = lower_solve(factor, lower_r.T).T
    basis_c = lower_solve(factor, lower_c.T).T
    top = lower_solve(factor, top_rows.T).T
    inverse = invert_shifted(jnp.eye(panel, dtype=jnp.float32) - top)
    embed_r = (row_global[:, None] == panel + span[None, :]).astype(jnp.float32)
    embed_c = (col_global[:, None] == panel + span[None, :]).astype(jnp.float32)
    reflect_r = basis_r - embed_r
    reflect_c = basis_c - embed_c
    stored = matrix[0, :, 0, :]
    col_select = (col_global[None, :] == span[:, None]).astype(jnp.float32)
    row_select = (row_global[None, :] == span[:, None]).astype(jnp.float32)
    left = jnp.dot(prow, col_select, precision=HIGH)
    upper = lax.dot_general(row_select, scols, (((0,), (1,)), ((), ())), precision=HIGH)
    inside_r = (row_global < panel)[:, None]
    inside_c = (col_global < panel)[None, :]
    refreshed = jnp.where(
        inside_r & inside_c,
        0.5 * (left + upper),
        jnp.where(inside_c, left, jnp.where(inside_r, upper, stored)),
    )
    zpart = jnp.dot(refreshed, reflect_c, precision=HIGH)
    zrows = sum_by_parts_2(zpart, "col")
    upart = lax.dot_general(refreshed, reflect_r, (((0,), (0,)), ((), ())), precision=HIGH)
    ucols = sum_by_parts_2(upart, "row")
    wmat = over_copies(jnp.dot(reflect_r.T, zrows, precision=HIGH), "row")
    core = jnp.dot(jnp.dot(inverse, wmat, precision=HIGH), inverse.T, precision=HIGH)
    first = jnp.dot(reflect_r, jnp.dot(inverse, ucols.T, precision=HIGH), precision=HIGH)
    second = jnp.dot(
        jnp.dot(zrows, inverse.T, precision=HIGH) - jnp.dot(reflect_r, core, precision=HIGH),
        reflect_c.T,
        precision=HIGH,
    )
    return (refreshed - first - second)[None, :, None, :]


def solution(mesh):
    in_specs = (
        P(("row", "col"), None),
        P(("row", "col"), None),
        P(("row", "col")),
        P("row", None, "col", None),
    )
    out_specs = P("row", None, "col", None)
    return jax.shard_map(
        per_device, mesh=mesh, in_specs=in_specs, out_specs=out_specs, check_vma=False
    )
```

profile of v0, /device:TPU:56, one launch (start us, length us, event | category | flops | bytes accessed | tf_op | source)
XLA Modules:
  0.0 485.3 jit_solution(14898159743396855273)
XLA Ops:
  6.5 0.0 all-reduce.2.cloned.1.call-start
  7.2 5.0 %convolution_bitcast_fusion = f32[8192,128]{0,1:T(8,128)} fusion(bf16[256,8192]{1,0:T(8,128)(2,1)} %param.7, bf16[256,128]{1,0:T(8,128)(2,1)} %param.8, pred[256]{0:T(512)(128)(4,1)S(1)} %iota_compare_fusion.9), kind=kOutput, calls=%fused_computation | convolution fusion | flops 536903680 | bytes 8454400 | tf_op jit(solution)/shard_map/dot_general | solution.py:99
  12.2 0.0 all-reduce.2.cloned.1.call-update
  12.4 291.1 %all-reduce.2.cloned.1.call-done = f32[8192,128]{0,1:T(8,128)} async-done(((f32[8192,128]{0,1:T(8,128)}), f32[8192,128]{0,1:T(8,128)}) %all-reduce.2.cloned.1.call-update) | async-done | bytes 4194320 | tf_op jit(solution)/shard_map/psum | solution.py:102
  303.5 5.6 %copy.21 = f32[8192,128]{1,0:T(8,128)} copy(f32[8192,128]{0,1:T(8,128)} %all-reduce.2.cloned.1.call-done) | data formatting | bytes 8388608 | tf_op jit(solution)/shard_map/psum | solution.py:102
  309.0 0.0 copy-start
  309.0 1.1 broadcast_select_fusion
  310.2 0.3 fusion.5
  310.5 0.6 convolution_bitcast_fusion.1
  311.2 0.7 all_to_all.25
  311.9 9.0 %all-to-all-start = ((f32[16,1,2048]{2,1,0:T(1,128)}), f32[16,1,2048]{2,1,0:T(1,128)S(1)}, u32[]{:S(2)}, u32[]{:S(2)}) async-start(f32[16,1,2048]{2,1,0:T(1,128)} %all_to_all.25), calls=%async_computation | async-start | bytes 262144 | tf_op jit(solution)/shard_map/all_to_all | solution.py:41
  320.9 1.0 broadcast_select_fusion.1
  321.9 0.4 fusion.11
  322.3 9.6 %all-to-all-done = f32[16,1,2048]{2,1,0:T(1,128)S(1)} async-done(((f32[16,1,2048]{2,1,0:T(1,128)}), f32[16,1,2048]{2,1,0:T(1,128)S(1)}, u32[]{:S(2)}, u32[]{:S(2)}) %all-to-all-start) | async-done | bytes 131104 | tf_op jit(solution)/shard_map/all_to_all | solution.py:41
  331.8 0.1 reduce_sum.36
  331.9 0.7 broadcast_in_dim.57
  332.6 5.0 %all-to-all-start.1 = ((f32[16,1,2048]{2,1,0:T(1,128)}), f32[16,1,2048]{2,1,0:T(1,128)S(1)}, u32[]{:S(2)}, u32[]{:S(2)}) async-start(f32[16,1,2048]{2,1,0:T(1,128)} %broadcast_in_dim.57), calls=%async_computation.1 | async-start | bytes 262144 | tf_op jit(solution)/shard_map/all_to_all | solution.py:25
  337.6 0.0 copy-done
  337.6 0.5 fusion.2
  338.1 10.5 %all-to-all-done.1 = f32[16,1,2048]{2,1,0:T(1,128)S(1)} async-done(((f32[16,1,2048]{2,1,0:T(1,128)}), f32[16,1,2048]{2,1,0:T(1,128)S(1)}, u32[]{:S(2)}, u32[]{:S(2)}) %all-to-all-start.1) | async-done | bytes 131104 | tf_op jit(solution)/shard_map/all_to_all | solution.py:25
  348.6 0.1 copy.23
  348.7 11.7 %cholesky.44 = f32[128,128]{1,0:T(8,128)S(1)} custom-call(f32[128,128]{1,0:T(8,128)S(1)} %fusion.24), custom_call_target="Cholesky" | custom-call | tf_op jit(solution)/shard_map/jit(cholesky)/cholesky | solution.py:116
  360.5 0.6 compare_reduce_fusion.1
  361.1 0.7 fusion.12
  361.8 9.8 %custom-call.13 = f32[1,128,128]{1,2,0:T(8,128)S(1)} custom-call(f32[1,128,128]{2,1,0:T(8,128)S(1)} %fusion.12), custom_call_target="InvertDiagBlocksLowerTriangular" | custom-call | tf_op jit(solution)/shard_map/triangular_solve | solution.py:72
  371.6 0.3 convolution_subtract_fusion.4
  371.9 1.3 fusion.73
  373.1 5.9 %all-to-all-start.4 = ((f32[32,16,128]{2,1,0:T(8,128)}), f32[32,16,128]{2,1,0:T(8,128)S(1)}, u32[]{:S(2)}, u32[]{:S(2)}) async-start(f32[32,16,128]{2,1,0:T(8,128)} %bitcast.26), calls=%async_computation.4 | async-start | bytes 524288 | tf_op jit(solution)/shard_map/all_to_all | solution.py:41
  379.1 0.4 convolution_subtract_fusion.3
  379.4 1.6 fusion.71
  381.1 8.4 %all-to-all-done.4 = f32[32,16,128]{2,1,0:T(8,128)S(1)} async-done(((f32[32,16,128]{2,1,0:T(8,128)}), f32[32,16,128]{2,1,0:T(8,128)S(1)}, u32[]{:S(2)}, u32[]{:S(2)}) %all-to-all-start.4) | async-done | bytes 262176 | tf_op jit(solution)/shard_map/all_to_all | solution.py:41
  389.5 5.1 %all-to-all-start.2 = ((f32[16,16,128]{2,1,0:T(8,128)}), f32[16,16,128]{2,1,0:T(8,128)S(1)}, u32[]{:S(2)}, u32[]{:S(2)}) async-start(f32[16,16,128]{2,1,0:T(8,128)} %bitcast.23), calls=%async_computation.2 | async-start | bytes 262144 | tf_op jit(solution)/shard_map/all_to_all | solution.py:41
  394.7 11.7 %all-to-all-done.2 = f32[16,16,128]{2,1,0:T(8,128)S(1)} async-done(((f32[16,16,128]{2,1,0:T(8,128)}), f32[16,16,128]{2,1,0:T(8,128)S(1)}, u32[]{:S(2)}, u32[]{:S(2)}) %all-to-all-start.2) | async-done | bytes 131104 | tf_op jit(solution)/shard_map/all_to_all | solution.py:41
  406.4 0.7 broadcast_in_dim.61
  407.2 4.4 all-to-all-start.5
  411.6 10.6 %all-to-all-done.5 = f32[32,16,128]{2,1,0:T(8,128)S(1)} async-done(((f32[32,16,128]{2,1,0:T(8,128)}), f32[32,16,128]{2,1,0:T(8,128)S(1)}, u32[]{:S(2)}, u32[]{:S(2)}) %all-to-all-start.5) | async-done | bytes 262176 | tf_op jit(solution)/shard_map/all_to_all | solution.py:25
  422.2 0.7 broadcast_in_dim.58
  422.9 4.8 all-to-all-start.3
  427.7 0.3 fusion.20
  428.0 0.6 fusion.75
  428.6 11.3 %all-to-all-done.3 = f32[16,16,128]{2,1,0:T(8,128)S(1)} async-done(((f32[16,16,128]{2,1,0:T(8,128)}), f32[16,16,128]{2,1,0:T(8,128)S(1)}, u32[]{:S(2)}, u32[]{:S(2)}) %all-to-all-start.3) | async-done | bytes 131104 | tf_op jit(solution)/shard_map/all_to_all | solution.py:25
  439.8 1.1 broadcast_in_dim.62
  440.9 4.6 all-to-all-start.6
  445.6 0.3 fusion.19
  445.8 0.1 copy.24
  445.9 11.7 %cholesky.55 = f32[128,128]{1,0:T(8,128)S(1)} custom-call(f32[128,128]{1,0:T(8,128)S(1)} %fusion.18), custom_call_target="Cholesky" | custom-call | tf_op jit(solution)/shard_map/jit(cholesky)/cholesky | solution.py:77
  457.7 0.6 compare_reduce_fusion
  458.3 0.7 fusion.13
  459.0 9.8 %custom-call.14 = f32[1,128,128]{1,2,0:T(8,128)S(1)} custom-call(f32[1,128,128]{2,1,0:T(8,128)S(1)} %fusion.13), custom_call_target="InvertDiagBlocksLowerTriangular" | custom-call | tf_op jit(solution)/shard_map/triangular_solve | solution.py:79
  468.8 0.3 fusion.14
  469.1 0.2 fusion.16
  469.3 0.3 fusion.72
  469.6 0.6 convolution_subtract_fusion.1
  470.2 0.4 fusion.74
  470.6 5.1 %all-to-all-done.6 = f32[16,128,128]{2,1,0:T(8,128)S(1)} async-done(((f32[16,128,128]{2,1,0:T(8,128)}), f32[16,128,128]{2,1,0:T(8,128)S(1)}, u32[]{:S(2)}, u32[]{:S(2)}) %all-to-all-start.6) | async-done | bytes 1048608 | tf_op jit(solution)/shard_map/all_to_all | solution.py:25
  475.6 0.1 reduce_sum.39
  475.7 0.2 fusion.76
  475.9 0.3 fusion.77
  476.2 0.4 convolution_subtract_fusion.2
  476.5 0.6 fusion
  477.1 1.3 copy.25
  (18 shorter events, 0.3 us)
Async XLA Ops:
  6.5 296.9 %all-reduce.2.cloned.1.call-start = ((), (), s32[]{:S(2)}) async-start(), calls=%async_computation.7 | async-start | bytes 8388608 | tf_op jit(solution)/shard_map/psum | solution.py:102
  309.0 28.6 %copy-start = (f32[1,512,1,256]{3,2,1,0:T(1,128)S(1)}, f32[1,512,1,256]{3,2,1,0:T(1,128)}, u32[]{:S(2)}) copy-start(f32[1,512,1,256]{3,2,1,0:T(1,128)} %param.10) | copy-start | bytes 1572868
  311.9 19.9 %all-to-all-start = ((f32[16,1,2048]{2,1,0:T(1,128)}), f32[16,1,2048]{2,1,0:T(1,128)S(1)}, u32[]{:S(2)}, u32[]{:S(2)}) async-start(f32[16,1,2048]{2,1,0:T(1,128)} %all_to_all.25), calls=%async_computation | async-start | bytes 262144 | tf_op jit(solution)/shard_map/all_to_all | solution.py:41
  332.6 15.9 %all-to-all-start.1 = ((f32[16,1,2048]{2,1,0:T(1,128)}), f32[16,1,2048]{2,1,0:T(1,128)S(1)}, u32[]{:S(2)}, u32[]{:S(2)}) async-start(f32[16,1,2048]{2,1,0:T(1,128)} %broadcast_in_dim.57), calls=%async_computation.1 | async-start | bytes 262144 | tf_op jit(solution)/shard_map/all_to_all | solution.py:25
  373.1 16.4 %all-to-all-start.4 = ((f32[32,16,128]{2,1,0:T(8,128)}), f32[32,16,128]{2,1,0:T(8,128)S(1)}, u32[]{:S(2)}, u32[]{:S(2)}) async-start(f32[32,16,128]{2,1,0:T(8,128)} %bitcast.26), calls=%async_computation.4 | async-start | bytes 524288 | tf_op jit(solution)/shard_map/all_to_all | solution.py:41
  389.5 16.9 %all-to-all-start.2 = ((f32[16,16,128]{2,1,0:T(8,128)}), f32[16,16,128]{2,1,0:T(8,128)S(1)}, u32[]{:S(2)}, u32[]{:S(2)}) async-start(f32[16,16,128]{2,1,0:T(8,128)} %bitcast.23), calls=%async_computation.2 | async-start | bytes 262144 | tf_op jit(solution)/shard_map/all_to_all | solution.py:41
  407.2 15.1 %all-to-all-start.5 = ((f32[32,16,128]{2,1,0:T(8,128)}), f32[32,16,128]{2,1,0:T(8,128)S(1)}, u32[]{:S(2)}, u32[]{:S(2)}) async-start(f32[32,16,128]{2,1,0:T(8,128)} %broadcast_in_dim.61), calls=%async_computation.5 | async-start | bytes 524288 | tf_op jit(solution)/shard_map/all_to_all | solution.py:25
  422.9 16.9 %all-to-all-start.3 = ((f32[16,16,128]{2,1,0:T(8,128)}), f32[16,16,128]{2,1,0:T(8,128)S(1)}, u32[]{:S(2)}, u32[]{:S(2)}) async-start(f32[16,16,128]{2,1,0:T(8,128)} %broadcast_in_dim.58), calls=%async_computation.3 | async-start | bytes 262144 | tf_op jit(solution)/shard_map/all_to_all | solution.py:25
  440.9 34.7 %all-to-all-start.6 = ((f32[16,128,128]{2,1,0:T(8,128)}), f32[16,128,128]{2,1,0:T(8,128)S(1)}, u32[]{:S(2)}, u32[]{:S(2)}) async-start(f32[16,128,128]{2,1,0:T(8,128)} %broadcast_in_dim.62), calls=%async_computation.6 | async-start | bytes 2097152 | tf_op jit(solution)/shard_map/all_to_all | solution.py:25
Sparse Core Ops, SparseCore 0:
  12.4 291.0 all-reduce.1
where the time goes:
time: 487 us; the launch traced here: 485 us
  waiting for transfers between devices  358 us (74%)
  other arithmetic  48.2 us (10%)
  starting transfers between devices  38.8 us (8%)
  matrix products  14.6 us (3%)
  between operations  14.4 us (3%)
  local copies, waits for them, and re-layouts  11.1 us (2%)
    psum x1, waiting for transfers between devices, per_device(): whole = lax.psum(partial_value, ('row', 'col'))  291 us
    all_to_all x4, waiting for transfers between devices, sent_to_all(): lax.all_to_all(jnp.broadcast_to(array[None], (devices, *array.shape)), ax...  37.4 us
    all_to_all x3, waiting for transfers between devices, summed_on_arrival(): lax.all_to_all(blocks, axis, split_axis=0, concat_axis=0, tiled=True)  29.7 us
    all_to_all x3, starting transfers between devices, summed_on_arrival(): lax.all_to_all(blocks, axis, split_axis=0, concat_axis=0, tiled=True)  20 us
    all_to_all x4, starting transfers between devices, sent_to_all(): lax.all_to_all(jnp.broadcast_to(array[None], (devices, *array.shape)), ax...  18.8 us
    another operation x3, other arithmetic, per_device(): factor = jnp.linalg.cholesky(gram)  12.4 us
    another operation x3, other arithmetic, invert_shifted(): factor = jnp.linalg.cholesky(normal)  12.4 us
    another operation x2, other arithmetic, lower_solve(): return lax.linalg.triangular_solve(factor, rhs, left_side=True, lower=True)  10.5 us
  transfers between devices with their start and end apart: 8, of which 8 were waited for; matrix products, arithmetic and copies ran while one was open for 6% of the time, Pallas kernels for 0%

commit v1 on v0

--- a/solution.py
+++ b/solution.py
@@ -2,6 +2,220 @@
 import jax.numpy as jnp
 from jax import lax
 from jax.sharding import PartitionSpec as P
+from jax.experimental import pallas as pl
+from jax.experimental.pallas import tpu as pltpu
+
+MESH = pl.DeviceIdType.MESH
+
+
+def position():
+    p, q = lax.axis_index("row"), lax.axis_index("col")
+    return p, q, p // 8, p % 8, q // 8, (q // 2) % 4, q % 2
+
+
+def device(zh, y, x, zl, c):
+    return (zh * 8 + y, x * 8 + zl * 2 + c)
+
+
+def send(src, dst, send_sem, recv_sem, target):
+    return pltpu.make_async_remote_copy(
+        src_ref=src, dst_ref=dst, send_sem=send_sem, recv_sem=recv_sem,
+        device_id=target, device_id_type=MESH,
+    )
+
+
+def panel_kernel(part, rows_out, cols_out, theirs, wa, wb, ra1, rb1, a1, b1, ra2, rb2,
+                 ab2, r3, own, ss, rs, ss_r, rs_r, ss_c, rs_c):
+    p, q, zh, y, x, zl, c = position()
+    z = zh * 4 + zl
+    first = c == 0
+    f = jnp.where(first, y, z)
+    s = jnp.where(first, z, y)
+
+    def at(xx, ff, sf):
+        yy, zz = jnp.where(first, ff, sf), jnp.where(first, sf, ff)
+        return device(zz // 4, yy, xx, zz % 4, c)
+
+    target_row = q % 16
+    tile = 2 * p + q // 16
+    partner = device(zh, y, x, zl, 1 - c)
+    barrier = pltpu.get_barrier_semaphore()
+
+    def hail(who):
+        pl.semaphore_signal(barrier, inc=1, device_id=who, device_id_type=MESH)
+
+    hail(partner)
+    for d in range(1, 4):
+        hail(at((x + d) % 4, f, s))
+    for d in range(1, 8):
+        hail(at(x, (f + d) % 8, s))
+        hail(at(x, f, (s + d) % 8))
+
+    def hail_row(d, _):
+        hail(((p + d) % 16, q))
+        return 0
+
+    lax.fori_loop(1, 16, hail_row, 0)
+
+    def hail_owner(i, _):
+        who_p, who_q = i // 2, p + 16 * (i % 2)
+
+        @pl.when((who_p != p) | (who_q != q))
+        def _():
+            hail((who_p, who_q))
+        return 0
+
+    lax.fori_loop(0, 32, hail_owner, 0)
+    pl.semaphore_wait(barrier, 1 + 3 + 7 + 7 + 15 + 31 + jnp.where(target_row != p, 1, 0))
+
+    swap = send(part.at[:, :, :, :, 1 - c], theirs, ss.at[0], rs.at[0], partner)
+    swap.start()
+    swap.wait()
+
+    def join(i, _):
+        ff, sf = i // 8, i % 8
+        yy, zz = jnp.where(first, ff, sf), jnp.where(first, sf, ff)
+        hh, ll = zz // 4, zz % 4
+        for xx in range(4):
+            total = part[hh, yy, xx, ll, c] + theirs[hh, yy, xx, ll]
+            wa[xx, ff, sf] = total[:8]
+            wb[ff, xx, sf] = total[8:]
+        return 0
+
+    lax.fori_loop(0, 64, join, 0)
+    copies_a, copies_b = [], []
+    for d in range(1, 4):
+        xx = (x + d) % 4
+        copies_a.append(send(wa.at[xx], ra1.at[d - 1], ss.at[d], rs.at[d], at(xx, f, s)))
+        copies_a[-1].start()
+    for d in range(1, 8):
+        ff = (f + d) % 8
+        copies_b.append(send(wb.at[ff], rb1.at[d - 1], ss.at[3 + d], rs.at[3 + d], at(x, ff, s)))
+        copies_b[-1].start()
+    for copy in copies_b:
+        copy.wait()
+
+    def sum_b1(i, _):
+        total = wb[f, i]
+        for d in range(7):
+            total += rb1[d, i]
+        b1[i] = total
+        return 0
+
+    lax.fori_loop(0, 4, sum_b1, 0)
+    copies_b = []
+    for d in range(1, 4):
+        xx = (x + d) % 4
+        copies_b.append(send(b1.at[xx], rb2.at[d - 1], ss.at[10 + d], rs.at[10 + d], at(xx, f, s)))
+        copies_b[-1].start()
+    for copy in copies_a:
+        copy.wait()
+
+    def sum_a1(i, _):
+        total = wa[x, i]
+        for d in range(3):
+            total += ra1[d, i]
+        a1[i] = total
+        return 0
+
+    lax.fori_loop(0, 8, sum_a1, 0)
+    copies_a = []
+    for d in range(1, 8):
+        ff = (f + d) % 8
+        copies_a.append(send(a1.at[ff], ra2.at[d - 1], ss.at[13 + d], rs.at[13 + d], at(x, ff, s)))
+        copies_a[-1].start()
+    for copy in copies_b:
+        copy.wait()
+    ab2[:, 1] = b1[x] + rb2[0] + rb2[1] + rb2[2]
+    for copy in copies_a:
+        copy.wait()
+    total = a1[f]
+    for d in range(7):
+        total += ra2[d]
+    ab2[:, 0] = total
+    copies = []
+    for d in range(1, 8):
+        sf = (s + d) % 8
+        copies.append(send(ab2.at[sf], r3.at[d - 1], ss.at[20 + d], rs.at[20 + d], at(x, f, sf)))
+        copies[-1].start()
+    for copy in copies:
+        copy.wait()
+    total = ab2[s]
+    for d in range(7):
+        total += r3[d]
+    own[...] = total.reshape(16, 128)
+    cols_out[p] = own[...]
+
+    def to_column(d):
+        return send(own, cols_out.at[p], ss_c.at[d], rs_c.at[p], ((p + d) % 16, q))
+
+    def to_row(d):
+        return send(own, rows_out.at[tile], ss_r.at[d], rs_r.at[tile], (target_row, (q + d) % 32))
+
+    for d in range(1, 16):
+        to_column(d).start()
+    for d in range(1, 32):
+        to_row(d).start()
+
+    @pl.when(target_row == p)
+    def _():
+        rows_out[tile] = own[...]
+
+    @pl.when(target_row != p)
+    def _():
+        to_row(0).start()
+
+    for d in range(1, 16):
+        to_column(d).wait_send()
+    for d in range(1, 32):
+        to_row(d).wait_send()
+
+    @pl.when(target_row != p)
+    def _():
+        to_row(0).wait_send()
+
+    for d in range(1, 16):
+        j = (p + d) % 16
+        send(own, cols_out.at[j], ss_c.at[d], rs_c.at[j], (j, q)).wait_recv()
+
+    def from_owner(i, _):
+        @pl.when((i // 2 != p) | (p + 16 * (i % 2) != q))
+        def _():
+            send(own, rows_out.at[i], ss_r.at[0], rs_r.at[i], (p, q)).wait_recv()
+        return 0
+
+    lax.fori_loop(0, 32, from_owner, 0)
+
+
+def panel_sum(part):
+    f32 = jnp.float32
+    vmem = pl.BlockSpec(memory_space=pltpu.VMEM)
+    dma = pltpu.SemaphoreType.DMA
+    rows, cols = pl.pallas_call(
+        panel_kernel,
+        name="panel_sum",
+        out_shape=(jax.ShapeDtypeStruct((32, 16, 128), f32), jax.ShapeDtypeStruct((16, 16, 128), f32)),
+        in_specs=[vmem],
+        out_specs=(vmem, vmem),
+        scratch_shapes=[
+            pltpu.VMEM((2, 8, 4, 4, 16, 128), f32),
+            pltpu.VMEM((4, 8, 8, 8, 128), f32),
+            pltpu.VMEM((8, 4, 8, 8, 128), f32),
+            pltpu.VMEM((3, 8, 8, 8, 128), f32),
+            pltpu.VMEM((7, 4, 8, 8, 128), f32),
+            pltpu.VMEM((8, 8, 8, 128), f32),
+            pltpu.VMEM((4, 8, 8, 128), f32),
+            pltpu.VMEM((7, 8, 8, 128), f32),
+            pltpu.VMEM((3, 8, 8, 128), f32),
+            pltpu.VMEM((8, 2, 8, 128), f32),
+            pltpu.VMEM((7, 2, 8, 128), f32),
+            pltpu.VMEM((16, 128), f32),
+            dma((28,)), dma((28,)), dma((32,)), dma((32,)), dma((16,)), dma((16,)),
+        ],
+        compiler_params=pltpu.CompilerParams(collective_id=1, has_side_effects=True, vmem_limit_bytes=48 << 20),
+    )(part.reshape(2, 8, 4, 4, 2, 16, 128))
+    return rows.reshape(512, 128), cols.reshape(256, 128)
+
 
 TILE = 16
 
@@ -99,13 +313,7 @@
     partial_value = lax.dot_general(
         psi, hcols, (((0,), (0,)), ((), ())), preferred_element_type=jnp.float32
     )
-    whole = lax.psum(partial_value, ("row", "col"))
-    prow = lax.dynamic_index_in_dim(
-        whole.reshape(tiles_r, n_row, TILE, panel), prow_id, 1, keepdims=False
-    ).reshape(local_rows, panel)
-    scols = lax.dynamic_index_in_dim(
-        whole.reshape(tiles_c, n_col, TILE, panel), pcol_id, 1, keepdims=False
-    ).reshape(local_cols, panel)
+    prow, scols = panel_sum(partial_value)
     span = jnp.arange(panel, dtype=jnp.int32)
     lower_r = jnp.where((row_global >= panel)[:, None], prow, jnp.zeros_like(prow))
     lower_c = jnp.where((col_global >= panel)[:, None], scols, jnp.zeros_like(scols))

time: 487 us -> 254 us (0.52)
  waiting for transfers between devices: 358 us -> 68.3 us
  Pallas kernels: 0 us -> 66.9 us
  between operations: 14.4 us -> 0.95 us
    psum x1 -> x0, waiting for transfers between devices: 291 us -> none  [per_device(): whole = lax.psum(partial_value, ('row', 'col'))]
    pallas_call x0 -> x1, Pallas kernels: none -> 66.9 us  [panel_sum(): pl.pallas_call(panel_kernel, name='panel_sum', out_shape=(jax.ShapeDtypeS...]
    dot_general x0 -> x1, local copies, waits for them, and re-layouts: none -> 5.57 us  [per_device(): lax.dot_general(psi, hcols, (((0,), (0,)), ((), ())), preferred_element_t...]
    psum x1 -> x0, local copies, waits for them, and re-layouts: 5.57 us -> none  [per_device(): whole = lax.psum(partial_value, ('row', 'col'))]
  transfers between devices with their start and end apart: 8 -> 7, of which waited for: 8 -> 7; matrix products, arithmetic and copies ran while one was open for 6% -> 11% of each run, Pallas kernels for 0% -> 0%
where the time goes in v1:
time: 254 us; the launch traced here: 253 us
  waiting for transfers between devices  68.3 us (27%)
  Pallas kernels  66.9 us (26%)
  other arithmetic  46.3 us (18%)
  starting transfers between devices  42.7 us (17%)
  matrix products  14.5 us (6%)
  local copies, waits for them, and re-layouts  13.3 us (5%)
    pallas_call x1, Pallas kernels, panel_sum(): pl.pallas_call(panel_kernel, name='panel_sum', out_shape=(jax.ShapeDtypeS...  66.9 us
    all_to_all x4, waiting for transfers between devices, sent_to_all(): lax.all_to_all(jnp.broadcast_to(array[None], (devices, *array.shape)), ax...  37.8 us
    all_to_all x3, waiting for transfers between devices, summed_on_arrival(): lax.all_to_all(blocks, axis, split_axis=0, concat_axis=0, tiled=True)  30.5 us
    all_to_all x3, starting transfers between devices, summed_on_arrival(): lax.all_to_all(blocks, axis, split_axis=0, concat_axis=0, tiled=True)  23.6 us
    all_to_all x4, starting transfers between devices, sent_to_all(): lax.all_to_all(jnp.broadcast_to(array[None], (devices, *array.shape)), ax...  19.1 us
    another operation x3, other arithmetic, per_device(): factor = jnp.linalg.cholesky(gram)  12.4 us
    another operation x3, other arithmetic, invert_shifted(): factor = jnp.linalg.cholesky(normal)  12.4 us
    another operation x2, other arithmetic, lower_solve(): return lax.linalg.triangular_solve(factor, rhs, left_side=True, lower=True)  10.5 us
  transfers between devices with their start and end apart: 7, of which 7 were waited for; matrix products, arithmetic and copies ran while one was open for 11% of the time, Pallas kernels for 0%

profile of v1, /device:TPU:56, one launch (start us, length us, event | category | flops | bytes accessed | tf_op | source)
XLA Modules:
  0.0 253.0 jit_solution(923150340517914455)
XLA Ops:
  0.7 5.0 %convolution_bitcast_fusion = f32[8192,128]{0,1:T(8,128)} fusion(bf16[256,8192]{1,0:T(8,128)(2,1)} %param.7, bf16[256,128]{1,0:T(8,128)(2,1)} %param.8, pred[256]{0:T(512)(128)(4,1)S(1)} %iota_compare_fusion.9), kind=kOutput, calls=%fused_computation | convolution fusion | flops 536903680 | bytes 8454400 | tf_op jit(solution)/shard_map/dot_general | solution.py:313
  5.7 5.6 %copy.21 = f32[8192,128]{1,0:T(8,128)} copy(f32[8192,128]{0,1:T(8,128)} %convolution_bitcast_fusion) | data formatting | bytes 8388608 | tf_op jit(solution)/shard_map/dot_general | solution.py:313
  11.3 0.0 copy-start
  11.3 2.2 copy-done
  13.5 0.0 copy-start.1
  13.5 66.9 %panel_sum.1 = (f32[32,16,128]{2,1,0:T(8,128)S(1)}, f32[16,16,128]{2,1,0:T(8,128)S(1)}) custom-call(f32[2,8,4,4,2,16,128]{6,5,4,3,2,1,0:T(8,128)S(1)} %bitcast.88), custom_call_target="tpu_custom_call" | custom-call | tf_op jit(solution)/shard_map/panel_sum/pallas_call | solution.py:194
  80.4 0.1 broadcast_select_fusion
  80.5 0.3 fusion.4
  80.8 0.6 convolution_bitcast_fusion.1
  81.5 0.7 all_to_all.25
  82.2 12.0 %all-to-all-start = ((f32[16,1,2048]{2,1,0:T(1,128)}), f32[16,1,2048]{2,1,0:T(1,128)S(1)}, u32[]{:S(2)}, u32[]{:S(2)}) async-start(f32[16,1,2048]{2,1,0:T(1,128)} %all_to_all.25), calls=%async_computation | async-start | bytes 262144 | tf_op jit(solution)/shard_map/all_to_all | solution.py:255
  94.3 0.4 fusion.10
  94.7 0.0 copy-done.1
  94.7 0.5 fusion.2
  95.2 10.1 %all-to-all-done = f32[16,1,2048]{2,1,0:T(1,128)S(1)} async-done(((f32[16,1,2048]{2,1,0:T(1,128)}), f32[16,1,2048]{2,1,0:T(1,128)S(1)}, u32[]{:S(2)}, u32[]{:S(2)}) %all-to-all-start) | async-done | bytes 131104 | tf_op jit(solution)/shard_map/all_to_all | solution.py:255
  105.3 0.1 reduce_sum.36
  105.4 0.7 broadcast_in_dim.57
  106.1 5.2 %all-to-all-start.1 = ((f32[16,1,2048]{2,1,0:T(1,128)}), f32[16,1,2048]{2,1,0:T(1,128)S(1)}, u32[]{:S(2)}, u32[]{:S(2)}) async-start(f32[16,1,2048]{2,1,0:T(1,128)} %broadcast_in_dim.57), calls=%async_computation.1 | async-start | bytes 262144 | tf_op jit(solution)/shard_map/all_to_all | solution.py:239
  111.4 0.1 broadcast_select_fusion.1
  111.5 10.8 %all-to-all-done.1 = f32[16,1,2048]{2,1,0:T(1,128)S(1)} async-done(((f32[16,1,2048]{2,1,0:T(1,128)}), f32[16,1,2048]{2,1,0:T(1,128)S(1)}, u32[]{:S(2)}, u32[]{:S(2)}) %all-to-all-start.1) | async-done | bytes 131104 | tf_op jit(solution)/shard_map/all_to_all | solution.py:239
  122.3 0.1 copy.22
  122.4 11.7 %cholesky.44 = f32[128,128]{1,0:T(8,128)S(1)} custom-call(f32[128,128]{1,0:T(8,128)S(1)} %fusion.23), custom_call_target="Cholesky" | custom-call | tf_op jit(solution)/shard_map/jit(cholesky)/cholesky | solution.py:324
  134.2 0.6 compare_reduce_fusion.1
  134.8 0.7 fusion.11
  135.5 9.8 %custom-call.13 = f32[1,128,128]{1,2,0:T(8,128)S(1)} custom-call(f32[1,128,128]{2,1,0:T(8,128)S(1)} %fusion.11), custom_call_target="InvertDiagBlocksLowerTriangular" | custom-call | tf_op jit(solution)/shard_map/triangular_solve | solution.py:286
  145.3 0.3 convolution_subtract_fusion.4
  145.6 1.3 fusion.72
  146.9 6.7 %all-to-all-start.4 = ((f32[32,16,128]{2,1,0:T(8,128)}), f32[32,16,128]{2,1,0:T(8,128)S(1)}, u32[]{:S(2)}, u32[]{:S(2)}) async-start(f32[32,16,128]{2,1,0:T(8,128)} %bitcast.24), calls=%async_computation.4 | async-start | bytes 524288 | tf_op jit(solution)/shard_map/all_to_all | solution.py:255
  153.6 0.4 convolution_subtract_fusion.3
  154.0 1.6 fusion.70
  155.6 8.6 %all-to-all-done.4 = f32[32,16,128]{2,1,0:T(8,128)S(1)} async-done(((f32[32,16,128]{2,1,0:T(8,128)}), f32[32,16,128]{2,1,0:T(8,128)S(1)}, u32[]{:S(2)}, u32[]{:S(2)}) %all-to-all-start.4) | async-done | bytes 262176 | tf_op jit(solution)/shard_map/all_to_all | solution.py:255
  164.3 4.9 %all-to-all-start.2 = ((f32[16,16,128]{2,1,0:T(8,128)}), f32[16,16,128]{2,1,0:T(8,128)S(1)}, u32[]{:S(2)}, u32[]{:S(2)}) async-start(f32[16,16,128]{2,1,0:T(8,128)} %bitcast.21), calls=%async_computation.2 | async-start | bytes 262144 | tf_op jit(solution)/shard_map/all_to_all | solution.py:255
  169.2 11.7 %all-to-all-done.2 = f32[16,16,128]{2,1,0:T(8,128)S(1)} async-done(((f32[16,16,128]{2,1,0:T(8,128)}), f32[16,16,128]{2,1,0:T(8,128)S(1)}, u32[]{:S(2)}, u32[]{:S(2)}) %all-to-all-start.2) | async-done | bytes 131104 | tf_op jit(solution)/shard_map/all_to_all | solution.py:255
  180.9 0.7 broadcast_in_dim.61
  181.6 4.4 %all-to-all-start.5 = ((f32[32,16,128]{2,1,0:T(8,128)}), f32[32,16,128]{2,1,0:T(8,128)S(1)}, u32[]{:S(2)}, u32[]{:S(2)}) async-start(f32[32,16,128]{2,1,0:T(8,128)} %broadcast_in_dim.61), calls=%async_computation.5 | async-start | bytes 524288 | tf_op jit(solution)/shard_map/all_to_all | solution.py:239
  186.1 10.6 %all-to-all-done.5 = f32[32,16,128]{2,1,0:T(8,128)S(1)} async-done(((f32[32,16,128]{2,1,0:T(8,128)}), f32[32,16,128]{2,1,0:T(8,128)S(1)}, u32[]{:S(2)}, u32[]{:S(2)}) %all-to-all-start.5) | async-done | bytes 262176 | tf_op jit(solution)/shard_map/all_to_all | solution.py:239
  196.7 0.7 broadcast_in_dim.58
  197.4 4.8 %all-to-all-start.3 = ((f32[16,16,128]{2,1,0:T(8,128)}), f32[16,16,128]{2,1,0:T(8,128)S(1)}, u32[]{:S(2)}, u32[]{:S(2)}) async-start(f32[16,16,128]{2,1,0:T(8,128)} %broadcast_in_dim.58), calls=%async_computation.3 | async-start | bytes 262144 | tf_op jit(solution)/shard_map/all_to_all | solution.py:239
  202.1 0.3 fusion.19
  202.4 0.6 fusion.74
  203.0 11.3 %all-to-all-done.3 = f32[16,16,128]{2,1,0:T(8,128)S(1)} async-done(((f32[16,16,128]{2,1,0:T(8,128)}), f32[16,16,128]{2,1,0:T(8,128)S(1)}, u32[]{:S(2)}, u32[]{:S(2)}) %all-to-all-start.3) | async-done | bytes 131104 | tf_op jit(solution)/shard_map/all_to_all | solution.py:239
  214.3 1.1 broadcast_in_dim.62
  215.4 4.6 %all-to-all-start.6 = ((f32[16,128,128]{2,1,0:T(8,128)}), f32[16,128,128]{2,1,0:T(8,128)S(1)}, u32[]{:S(2)}, u32[]{:S(2)}) async-start(f32[16,128,128]{2,1,0:T(8,128)} %broadcast_in_dim.62), calls=%async_computation.6 | async-start | bytes 2097152 | tf_op jit(solution)/shard_map/all_to_all | solution.py:239
  220.0 0.3 fusion.18
  220.3 0.1 copy.23
  220.4 11.7 %cholesky.55 = f32[128,128]{1,0:T(8,128)S(1)} custom-call(f32[128,128]{1,0:T(8,128)S(1)} %fusion.17), custom_call_target="Cholesky" | custom-call | tf_op jit(solution)/shard_map/jit(cholesky)/cholesky | solution.py:291
  232.2 0.6 compare_reduce_fusion
  232.8 0.7 fusion.12
  233.5 9.8 %custom-call.14 = f32[1,128,128]{1,2,0:T(8,128)S(1)} custom-call(f32[1,128,128]{2,1,0:T(8,128)S(1)} %fusion.12), custom_call_target="InvertDiagBlocksLowerTriangular" | custom-call | tf_op jit(solution)/shard_map/triangular_solve | solution.py:293
  243.3 0.3 fusion.13
  243.6 0.2 fusion.15
  243.8 0.3 fusion.71
  244.1 0.6 convolution_subtract_fusion.1
  244.6 0.4 fusion.73
  245.0 5.1 %all-to-all-done.6 = f32[16,128,128]{2,1,0:T(8,128)S(1)} async-done(((f32[16,128,128]{2,1,0:T(8,128)}), f32[16,128,128]{2,1,0:T(8,128)S(1)}, u32[]{:S(2)}, u32[]{:S(2)}) %all-to-all-start.6) | async-done | bytes 1048608 | tf_op jit(solution)/shard_map/all_to_all | solution.py:239
  250.1 0.1 reduce_sum.39
  250.2 0.2 fusion.75
  250.4 0.3 fusion.76
  250.7 0.4 convolution_subtract_fusion.2
  251.0 0.6 fusion
  251.6 1.3 copy.24
  (18 shorter events, 0.3 us)
Async XLA Ops:
  11.3 2.2 copy-start
  13.5 81.2 %copy-start.1 = (f32[1,512,1,256]{3,2,1,0:T(1,128)S(1)}, f32[1,512,1,256]{3,2,1,0:T(1,128)}, u32[]{:S(2)}) copy-start(f32[1,512,1,256]{3,2,1,0:T(1,128)} %param.10) | copy-start | bytes 1572868
  82.2 23.1 %all-to-all-start = ((f32[16,1,2048]{2,1,0:T(1,128)}), f32[16,1,2048]{2,1,0:T(1,128)S(1)}, u32[]{:S(2)}, u32[]{:S(2)}) async-start(f32[16,1,2048]{2,1,0:T(1,128)} %all_to_all.25), calls=%async_computation | async-start | bytes 262144 | tf_op jit(solution)/shard_map/all_to_all | solution.py:255
  106.1 16.2 %all-to-all-start.1 = ((f32[16,1,2048]{2,1,0:T(1,128)}), f32[16,1,2048]{2,1,0:T(1,128)S(1)}, u32[]{:S(2)}, u32[]{:S(2)}) async-start(f32[16,1,2048]{2,1,0:T(1,128)} %broadcast_in_dim.57), calls=%async_computation.1 | async-start | bytes 262144 | tf_op jit(solution)/shard_map/all_to_all | solution.py:239
  146.9 17.4 %all-to-all-start.4 = ((f32[32,16,128]{2,1,0:T(8,128)}), f32[32,16,128]{2,1,0:T(8,128)S(1)}, u32[]{:S(2)}, u32[]{:S(2)}) async-start(f32[32,16,128]{2,1,0:T(8,128)} %bitcast.24), calls=%async_computation.4 | async-start | bytes 524288 | tf_op jit(solution)/shard_map/all_to_all | solution.py:255
  164.3 16.7 %all-to-all-start.2 = ((f32[16,16,128]{2,1,0:T(8,128)}), f32[16,16,128]{2,1,0:T(8,128)S(1)}, u32[]{:S(2)}, u32[]{:S(2)}) async-start(f32[16,16,128]{2,1,0:T(8,128)} %bitcast.21), calls=%async_computation.2 | async-start | bytes 262144 | tf_op jit(solution)/shard_map/all_to_all | solution.py:255
  181.6 15.1 %all-to-all-start.5 = ((f32[32,16,128]{2,1,0:T(8,128)}), f32[32,16,128]{2,1,0:T(8,128)S(1)}, u32[]{:S(2)}, u32[]{:S(2)}) async-start(f32[32,16,128]{2,1,0:T(8,128)} %broadcast_in_dim.61), calls=%async_computation.5 | async-start | bytes 524288 | tf_op jit(solution)/shard_map/all_to_all | solution.py:239
  197.4 16.9 %all-to-all-start.3 = ((f32[16,16,128]{2,1,0:T(8,128)}), f32[16,16,128]{2,1,0:T(8,128)S(1)}, u32[]{:S(2)}, u32[]{:S(2)}) async-start(f32[16,16,128]{2,1,0:T(8,128)} %broadcast_in_dim.58), calls=%async_computation.3 | async-start | bytes 262144 | tf_op jit(solution)/shard_map/all_to_all | solution.py:239
  215.4 34.7 %all-to-all-start.6 = ((f32[16,128,128]{2,1,0:T(8,128)}), f32[16,128,128]{2,1,0:T(8,128)S(1)}, u32[]{:S(2)}, u32[]{:S(2)}) async-start(f32[16,128,128]{2,1,0:T(8,128)} %broadcast_in_dim.62), calls=%async_computation.6 | async-start | bytes 2097152 | tf_op jit(solution)/shard_map/all_to_all | solution.py:239

commit v2 on v1

v2 whole, which is shorter than its diff:
```python
import jax
import jax.numpy as jnp
from jax import lax
from jax.sharding import PartitionSpec as P
from jax.experimental import pallas as pl
from jax.experimental.pallas import tpu as pltpu

MESH = pl.DeviceIdType.MESH
HIGH = lax.Precision.HIGHEST
F32, BF16 = jnp.float32, jnp.bfloat16


def position():
    p, q = lax.axis_index("row"), lax.axis_index("col")
    return p, q, p // 8, p % 8, q // 8, (q // 2) % 4, q % 2


def device(zh, y, x, zl, c):
    return (zh * 8 + y, x * 8 + zl * 2 + c)


def send(src, dst, send_sem, recv_sem, target):
    return pltpu.make_async_remote_copy(
        src_ref=src, dst_ref=dst, send_sem=send_sem, recv_sem=recv_sem,
        device_id=target, device_id_type=MESH,
    )


def dot(a, b, ca, cb, precision=None):
    return lax.dot_general(
        a, b, (((ca,), (cb,)), ((), ())), precision=precision, preferred_element_type=F32
    )


def halves(a):
    high = a.astype(BF16)
    return high, (a - high.astype(F32)).astype(BF16)


def dot3(a, b, ca, cb):
    (ah, al), (bh, bl) = halves(a), halves(b)
    return dot(ah, bh, ca, cb) + (dot(ah, bl, ca, cb) + dot(al, bh, ca, cb))


def thirds(a):
    high = a.astype(BF16).astype(F32)
    rest = a - high
    middle = rest.astype(BF16).astype(F32)
    return high, middle, rest - middle


def outer(a, b):
    (ah, am, al), (bh, bm, bl) = thirds(a), thirds(b)
    left = jnp.concatenate([ah, ah, am, am, ah, al], 0).astype(BF16)
    right = jnp.concatenate([bh, bm, bh, bm, bl, bh], 0).astype(BF16)
    return dot(left, right, 0, 0)


def spread_columns(rows, base):
    turned = pltpu.roll(rows, (128 - base) % 128, 1)
    return [jnp.broadcast_to(turned[:, j : j + 1], (8, 128)) for j in range(8)]


def cholesky_block(k, a, ut):
    base = pl.multiple_of(8 * k, 8)
    sub = lax.broadcasted_iota(jnp.int32, (8, 128), 0)
    lane = lax.broadcasted_iota(jnp.int32, (8, 128), 1)
    rows = a[pl.ds(base, 8), :]
    cols = spread_columns(rows, base)
    for j in range(8):
        pivot = cols[j][j : j + 1]
        inv = lax.rsqrt(pivot)
        inv = inv * (1.5 - 0.5 * pivot * inv * inv)
        unit = rows[j : j + 1] * inv
        factor = jnp.where(sub > j, cols[j] * inv, 0.0)
        rows = jnp.where(sub == j, unit, rows - factor * unit)
        for i in range(j + 1, 8):
            cols[i] = cols[i] - factor * (cols[i][j : j + 1] * inv)
    done = jnp.where(lane >= base + sub, rows, 0.0)
    ut[pl.ds(base, 8), :] = done
    a[...] -= outer(done, done)


def inverse_block(k, n, t, lower, upper):
    base = pl.multiple_of(8 * k, 8)
    sub = lax.broadcasted_iota(jnp.int32, (8, 128), 0)
    rows, turned = n[pl.ds(base, 8), :], t[pl.ds(base, 8), :]
    rc, tc = spread_columns(rows[:, :128], base), spread_columns(turned[:, :128], base)
    scale = jnp.zeros((8, 128), F32)
    for j in range(8):
        inv = 1.0 / rc[j][j : j + 1]
        scale = jnp.where(sub == j, inv, scale)
        down = jnp.where(sub > j, rc[j] * inv, 0.0)
        across = jnp.where(sub > j, tc[j] * inv, 0.0)
        rows = rows - jnp.concatenate([down, down], 1) * rows[j : j + 1]
        turned = turned - jnp.concatenate([across, across], 1) * turned[j : j + 1]
        for i in range(j + 1, 8):
            rc[i] = rc[i] - down * rc[i][j : j + 1]
            tc[i] = tc[i] - across * tc[i][j : j + 1]
    turned = turned * jnp.concatenate([scale, scale], 1)
    lower[pl.ds(base, 8), :] = rows[:, 128:]
    upper[pl.ds(base, 8), :] = turned[:, 128:]
    n[...] -= outer(turned[:, :128], rows)
    t[...] -= outer(rows[:, :128], turned)


def step_kernel(part, stored, out, theirs, wa, wb, ra1, rb1, a1, b1, ra2, rb2, ab2, r3, own,
                srow, scol, mh, slr, slc, small, gx, gfull, s1, m1c, m1r, xpart, xin, xown,
                xr, xc, work, ut, n, t, lower, upper, zr, zc, wx, wfull, piece,
                ss, rs, ss_r, rs_r, ss_c, rs_c, ss_g, rs_g, ss_h, rs_h, ss_s, rs_s,
                ss_m, rs_m, ss_k, rs_k, ss_x, rs_x, ss_y, rs_y, ss_z, rs_z,
                ss_w, rs_w, ss_v, rs_v):
    p, q, zh, y, x, zl, c = position()
    z = zh * 4 + zl
    first = c == 0
    f = jnp.where(first, y, z)
    s = jnp.where(first, z, y)
    half, slot = q // 16, q % 16
    on_diagonal = slot == p
    piece_at = q // 2

    def at(xx, ff, sf):
        yy, zz = jnp.where(first, ff, sf), jnp.where(first, sf, ff)
        return device(zz // 4, yy, xx, zz % 4, c)

    def loop(start, stop, body):
        def step(i, carry):
            body(i)
            return carry
        lax.fori_loop(start, stop, step, 0)

    partner = device(zh, y, x, zl, 1 - c)
    barrier = pltpu.get_barrier_semaphore()

    def hail(who):
        pl.semaphore_signal(barrier, inc=1, device_id=who, device_id_type=MESH)

    def hail_unless_me(who):
        @pl.when((who[0] != p) | (who[1] != q))
        def _():
            hail(who)

    hail(partner)
    for d in range(1, 4):
        hail(at((x + d) % 4, f, s))
    for d in range(1, 8):
        hail(at(x, (f + d) % 8, s))
        hail(at(x, f, (s + d) % 8))
    loop(1, 16, lambda d: hail(((p + d) % 16, q)))
    loop(1, 32, lambda d: hail((p, (q + d) % 32)))
    loop(0, 32, lambda i: hail_unless_me((i % 16, p + 16 * (i // 16))))
    loop(0, 16, lambda j: hail_unless_me((slot, 16 * half + j)))
    pl.semaphore_wait(barrier, 18 + 15 + 31 + 31 + 15 + 2 * jnp.where(on_diagonal, 0, 1))

    swap = send(part.at[:, :, :, :, 1 - c], theirs, ss.at[0], rs.at[0], partner)
    swap.start()
    swap.wait()

    def join(i, _):
        ff, sf = i // 8, i % 8
        yy, zz = jnp.where(first, ff, sf), jnp.where(first, sf, ff)
        hh, ll = zz // 4, zz % 4
        for xx in range(4):
            total = part[hh, yy, xx, ll, c] + theirs[hh, yy, xx, ll]
            wa[xx, ff, sf] = total[:8]
            wb[ff, xx, sf] = total[8:]
        return 0

    lax.fori_loop(0, 64, join, 0)
    copies_a, copies_b = [], []
    for d in range(1, 4):
        xx = (x + d) % 4
        copies_a.append(send(wa.at[xx], ra1.at[d - 1], ss.at[d], rs.at[d], at(xx, f, s)))
        copies_a[-1].start()
    for d in range(1, 8):
        ff = (f + d) % 8
        copies_b.append(send(wb.at[ff], rb1.at[d - 1], ss.at[3 + d], rs.at[3 + d], at(x, ff, s)))
        copies_b[-1].start()
    for copy in copies_b:
        copy.wait()

    def sum_b1(i, _):
        total = wb[f, i]
        for d in range(7):
            total += rb1[d, i]
        b1[i] = total
        return 0

    lax.fori_loop(0, 4, sum_b1, 0)
    copies_b = []
    for d in range(1, 4):
        xx = (x + d) % 4
        copies_b.append(send(b1.at[xx], rb2.at[d - 1], ss.at[10 + d], rs.at[10 + d], at(xx, f, s)))
        copies_b[-1].start()
    for copy in copies_a:
        copy.wait()

    def sum_a1(i, _):
        total = wa[x, i]
        for d in range(3):
            total += ra1[d, i]
        a1[i] = total
        return 0

    lax.fori_loop(0, 8, sum_a1, 0)
    copies_a = []
    for d in range(1, 8):
        ff = (f + d) % 8
        copies_a.append(send(a1.at[ff], ra2.at[d - 1], ss.at[13 + d], rs.at[13 + d], at(x, ff, s)))
        copies_a[-1].start()
    for copy in copies_b:
        copy.wait()
    ab2[:, 1] = b1[x] + rb2[0] + rb2[1] + rb2[2]
    for copy in copies_a:
        copy.wait()
    total = a1[f]
    for d in range(7):
        total += ra2[d]
    ab2[:, 0] = total
    copies = []
    for d in range(1, 8):
        sf = (s + d) % 8
        copies.append(send(ab2.at[sf], r3.at[d - 1], ss.at[20 + d], rs.at[20 + d], at(x, f, sf)))
        copies[-1].start()
    for copy in copies:
        copy.wait()
    total = ab2[s]
    for d in range(7):
        total += r3[d]
    own[...] = total.reshape(16, 128)
    scol[p] = own[...]

    def to_row_group(src, dst, sem, landed):
        return lambda d: send(src, dst, sem.at[d], landed, ((p + d) % 16, q))

    def to_col_group(src, dst, sem, landed):
        return lambda d: send(src, dst, sem.at[d], landed, (p, (q + d) % 32))

    def start_all(copy, stop):
        loop(1, stop, lambda d: copy(d).start())

    def sent_all(copy, stop):
        loop(1, stop, lambda d: copy(d).wait_send())

    def landed(dst, sem):
        send(dst, dst, ss.at[0], sem, (p, q)).wait_recv()

    put_c = to_row_group(own, scol.at[p], ss_c, rs_c.at[p])
    row_slot = 16 * half + p

    def put_r(d):
        return send(own, srow.at[row_slot], ss_r.at[d], rs_r.at[row_slot], (slot, (q + d) % 32))

    start_all(put_c, 16)
    start_all(put_r, 32)

    @pl.when(on_diagonal)
    def _():
        srow[row_slot] = own[...]

    @pl.when(jnp.logical_not(on_diagonal))
    def _():
        put_r(0).start()

    loop(1, 16, lambda d: landed(scol.at[(p + d) % 16], rs_c.at[(p + d) % 16]))

    def take_row(i):
        @pl.when((i % 16 != p) | (p + 16 * (i // 16) != q))
        def _():
            landed(srow.at[i], rs_r.at[i])

    loop(0, 32, take_row)

    lane = lax.broadcasted_iota(jnp.int32, (16, 128), 1)
    in_left = (lane < 16) & (q < 8)
    zero = jnp.zeros((16, 128), F32)

    def refresh(i):
        tile = srow[i]
        slr[i] = jnp.where((i == 0) & (p < 8), zero, tile)
        left = pltpu.roll(tile, (128 - 16 * (q % 8)) % 128, 1)
        old = stored[2 * (i % 16) + i // 16]
        mh[i, :, :128] = jnp.where(in_left, left, old[:, :128])
        mh[i, :, 128:] = old[:, 128:]

    loop(0, 32, refresh)
    slc[...] = scol[...]

    @pl.when(q < 8)
    def _():
        slc[0] = zero

    @pl.when(p < 8)
    def _():
        turned = pltpu.roll(scol[...].reshape(256, 128), (128 - 16 * (p % 8)) % 128, 1)
        upper_rows = turned.T[:16]
        mh[0, :, :128] = jnp.where(
            in_left, 0.5 * (mh[0, :, :128] + upper_rows[:, :128]), upper_rows[:, :128]
        )
        mh[0, :, 128:] = upper_rows[:, 128:]

    low = slr[...].reshape(512, 128)
    small[...] = dot(low, low, 0, 0, HIGH)
    gx[p] = small[pl.ds(pl.multiple_of(8 * piece_at, 8), 8), :]
    put_g = to_row_group(gx.at[p], gx.at[p], ss_g, rs_g.at[p])
    start_all(put_g, 16)
    from_panel = jnp.maximum(p - 8, 0)
    put_s = to_row_group(srow.at[0], s1.at[from_panel], ss_s, rs_s.at[from_panel])

    @pl.when(p >= 8)
    def _():
        s1[from_panel] = srow[0]
        start_all(put_s, 16)

    xpart[...] = dot3(mh[...].reshape(512, 256), slc[...].reshape(256, 128), 1, 0).reshape(32, 16, 128)

    def put_x(d):
        to = (q + d) % 32
        return send(xpart.at[to], xin.at[q], ss_x.at[d], rs_x.at[q], (p, to))

    start_all(put_x, 32)
    put_m = to_row_group(mh.at[0], m1c.at[from_panel], ss_m, rs_m.at[from_panel])
    rim = 8 * half + from_panel

    def put_k(d):
        return send(mh.at[0], m1r.at[rim], ss_k.at[d], rs_k.at[rim], (slot, (q + d) % 32))

    @pl.when(p >= 8)
    def _():
        m1c[from_panel] = mh[0]

    @pl.when((p >= 8) & on_diagonal)
    def _():
        m1r[rim] = mh[0]

    def all_landed(buffer, sem, count, me):
        loop(1, count, lambda d: landed(buffer.at[(me + d) % count], sem.at[(me + d) % count]))

    def total_of(buffer, count):
        total = buffer[0]
        for i in range(1, count):
            total += buffer[i]
        return total

    def put_piece(full, sem, got):
        def copy(d):
            to = (piece_at + d) % 16
            return send(full.at[piece_at], full.at[piece_at], sem.at[d], got.at[piece_at], (p, 2 * to + c))
        return copy

    all_landed(gx, rs_g, 16, p)
    gfull[piece_at] = total_of(gx, 16)
    put_h = put_piece(gfull, ss_h, rs_h)
    start_all(put_h, 16)

    all_landed(xin, rs_x, 32, q)
    xin[q] = xpart[q]
    xown[...] = total_of(xin, 32)
    xr[q] = xown[...]
    put_y = to_col_group(xown, xr.at[q], ss_y, rs_y.at[q])
    start_all(put_y, 32)

    def put_z(d):
        return send(xown, xc.at[slot], ss_z.at[d], rs_z.at[slot], ((p + d) % 16, p + 16 * half))

    start_all(put_z, 16)

    @pl.when(on_diagonal)
    def _():
        xc[slot] = xown[...]

    @pl.when(jnp.logical_not(on_diagonal))
    def _():
        put_z(0).start()

    @pl.when(p >= 8)
    def _():
        start_all(put_k, 32)
        start_all(put_m, 16)

    @pl.when((p >= 8) & jnp.logical_not(on_diagonal))
    def _():
        put_k(0).start()

    all_landed(gfull, rs_h, 16, piece_at)
    gram = gfull[...].reshape(128, 128)
    work[...] = gram
    loop(0, 16, lambda k: cholesky_block(k, work, ut))

    def take_from_panel(i):
        @pl.when(i + 8 != p)
        def _():
            landed(s1.at[i], rs_s.at[i])
            landed(m1c.at[i], rs_m.at[i])

    loop(0, 8, take_from_panel)
    tops = s1[...].reshape(128, 128)
    normal = gram - dot(ut[...], tops, 0, 0, HIGH)
    eye = (
        lax.broadcasted_iota(jnp.int32, (128, 128), 0) == lax.broadcasted_iota(jnp.int32, (128, 128), 1)
    ).astype(F32)
    n[:, :128] = normal
    n[:, 128:] = eye
    t[:, :128] = normal.T
    t[:, 128:] = eye

    @pl.when(p >= 8)
    def _():
        slr[0] -= ut[pl.ds(pl.multiple_of(16 * from_panel, 16), 16), :]

    @pl.when((q >= 8) & (q < 16))
    def _():
        slc[0] -= ut[pl.ds(pl.multiple_of(16 * jnp.clip(q - 8, 0, 7), 16), 16), :]

    all_landed(xr, rs_y, 32, q)

    def take_xc(j):
        @pl.when((slot != p) | (16 * half + j != q))
        def _():
            landed(xc.at[j], rs_z.at[j])

    loop(0, 16, take_xc)

    def take_rim(i):
        @pl.when((i % 8 + 8 != p) | (p + 16 * (i // 8) != q))
        def _():
            landed(m1r.at[i], rs_k.at[i])

    loop(0, 16, take_rim)
    root = ut[...]
    for h in range(2):
        zr[pl.ds(256 * h, 256), :] = xr[pl.ds(16 * h, 16)].reshape(256, 128) - dot3(
            m1r[pl.ds(8 * h, 8)].reshape(128, 256), root, 0, 0
        )
    zc[...] = xc[...].reshape(256, 128) - dot3(m1c[...].reshape(128, 256), root, 0, 0)
    small[...] = dot3(slr[...].reshape(512, 128), zr[...], 0, 0)
    wx[p] = small[pl.ds(pl.multiple_of(8 * piece_at, 8), 8), :]
    put_w = to_row_group(wx.at[p], wx.at[p], ss_w, rs_w.at[p])
    start_all(put_w, 16)
    loop(0, 10, lambda k: inverse_block(k, n, t, lower, upper))
    all_landed(wx, rs_w, 16, p)
    wfull[piece_at] = total_of(wx, 16)
    put_v = put_piece(wfull, ss_v, rs_v)
    start_all(put_v, 16)
    loop(10, 16, lambda k: inverse_block(k, n, t, lower, upper))
    inverse_t = dot(lower[...], upper[...], 0, 0, HIGH)
    small[...] = inverse_t
    acols = dot3(zc[...], inverse_t, 1, 0)
    all_landed(wfull, rs_v, 16, piece_at)
    core = dot(
        dot(small[...], wfull[...].reshape(128, 128), 0, 0, HIGH), small[...], 1, 0, HIGH
    )
    right = jnp.concatenate([acols, slc[...].reshape(256, 128)], 1)
    rh, rl = halves(right)
    for h in range(4):
        rows = slr[pl.ds(8 * h, 8)].reshape(128, 128)
        brows = dot3(zr[pl.ds(128 * h, 128), :], small[...], 1, 0) - dot3(rows, core, 1, 0)
        lh, ll = halves(jnp.concatenate([rows, brows], 1))
        change = dot(lh, rh, 1, 1) + (dot(lh, rl, 1, 1) + dot(ll, rh, 1, 1))
        for i in range(8):
            at_tile = 8 * h + i
            out[2 * (at_tile % 16) + at_tile // 16] = mh[at_tile] - change[16 * i : 16 * i + 16]

    sent_all(put_c, 16)
    sent_all(put_r, 32)
    sent_all(put_g, 16)
    sent_all(put_h, 16)
    sent_all(put_x, 32)
    sent_all(put_y, 32)
    sent_all(put_z, 16)
    sent_all(put_w, 16)
    sent_all(put_v, 16)

    @pl.when(jnp.logical_not(on_diagonal))
    def _():
        put_r(0).wait_send()
        put_z(0).wait_send()

    @pl.when(p >= 8)
    def _():
        sent_all(put_s, 16)
        sent_all(put_m, 16)
        sent_all(put_k, 32)

    @pl.when((p >= 8) & jnp.logical_not(on_diagonal))
    def _():
        put_k(0).wait_send()


def step(part, stored):
    vmem = pl.BlockSpec(memory_space=pltpu.VMEM)

    def room(*dims):
        return pltpu.VMEM(dims, F32)

    sems = [28, 28, 32, 32, 16, 16, 16, 16, 16, 16, 16, 8, 16, 8, 32, 16, 32, 32, 32, 32, 16, 16, 16, 16, 16, 16]
    return pl.pallas_call(
        step_kernel,
        name="step",
        out_shape=jax.ShapeDtypeStruct((32, 16, 256), F32),
        in_specs=[vmem, vmem],
        out_specs=vmem,
        scratch_shapes=[
            room(2, 8, 4, 4, 16, 128), room(4, 8, 8, 8, 128), room(8, 4, 8, 8, 128),
            room(3, 8, 8, 8, 128), room(7, 4, 8, 8, 128), room(8, 8, 8, 128), room(4, 8, 8, 128),
            room(7, 8, 8, 128), room(3, 8, 8, 128), room(8, 2, 8, 128), room(7, 2, 8, 128),
            room(16, 128),
            room(32, 16, 128), room(16, 16, 128), room(32, 16, 256), room(32, 16, 128),
            room(16, 16, 128), room(128, 128), room(16, 8, 128), room(16, 8, 128),
            room(8, 16, 128), room(8, 16, 256), room(16, 16, 256), room(32, 16, 128),
            room(32, 16, 128), room(16, 128), room(32, 16, 128), room(16, 16, 128),
            room(128, 128), room(128, 128), room(128, 256), room(128, 256), room(128, 128),
            room(128, 128), room(512, 128), room(256, 128), room(16, 8, 128), room(16, 8, 128),
            room(8, 128),
        ] + [pltpu.SemaphoreType.DMA((k,)) for k in sems],
        compiler_params=pltpu.CompilerParams(
            collective_id=1, has_side_effects=True, vmem_limit_bytes=56 << 20
        ),
    )(part.reshape(2, 8, 4, 4, 2, 16, 128), stored)


def per_device(psi, hpsi, slab_counts, matrix):
    slots = psi.shape[0]
    valid = jnp.arange(slots, dtype=jnp.int32) < slab_counts[0]
    hcols = jnp.where(valid[:, None], hpsi, jnp.zeros_like(hpsi))
    part = dot(psi, hcols, 0, 0)
    return step(part, matrix.reshape(32, 16, 256)).reshape(matrix.shape)


def solution(mesh):
    in_specs = (
        P(("row", "col"), None),
        P(("row", "col"), None),
        P(("row", "col")),
        P("row", None, "col", None),
    )
    out_specs = P("row", None, "col", None)
    return jax.shard_map(
        per_device, mesh=mesh, in_specs=in_specs, out_specs=out_specs, check_vma=False
    )
```

time: 254 us -> 180 us (0.71)
  Pallas kernels: 66.9 us -> 162 us
  waiting for transfers between devices: 68.3 us -> 0 us
  other arithmetic: 46.3 us -> 0.01 us
  starting transfers between devices: 42.7 us -> 0 us
  matrix products: 14.5 us -> 5.03 us
  local copies, waits for them, and re-layouts: 13.3 us -> 8.83 us
    pallas_call x1, Pallas kernels: 66.9 us -> 162 us  [step(): pl.pallas_call(step_kernel, name='step', out_shape=jax.ShapeDtypeStruct((...]
    all_to_all x7 -> x0, waiting for transfers between devices: 68.3 us -> none  [the longest x4 37.8 us: sent_to_all(): lax.all_to_all(jnp.broadcast_to(array[None], (devices, *array.shape)), ax...]
    another operation x10 -> x0, other arithmetic: 45.7 us -> none  [the longest x3 12.4 us: per_device(): factor = jnp.linalg.cholesky(gram)]
    all_to_all x7 -> x0, starting transfers between devices: 42.7 us -> none  [the longest x3 23.6 us: summed_on_arrival(): lax.all_to_all(blocks, axis, split_axis=0, concat_axis=0, tiled=True)]
    dot_general x16 -> x1, matrix products: 13.1 us -> 5.03 us  [dot(): lax.dot_general(a, b, (((ca,), (cb,)), ((), ())), precision=precision, pr...]
    broadcast_in_dim x5 -> x0, local copies, waits for them, and re-layouts: 4.53 us -> none  [the longest x4 3.2 us: sent_to_all(): jnp.broadcast_to(array[None], (devices, *array.shape))]
    dot_general x2 -> x1, local copies, waits for them, and re-layouts: 5.66 us -> 5.63 us  [dot(): lax.dot_general(a, b, (((ca,), (cb,)), ((), ())), precision=precision, pr...]
  transfers between devices with their start and end apart: 7 -> 0, of which waited for: 7 -> 0; matrix products, arithmetic and copies ran while one was open for 11% -> 0% of each run, Pallas kernels for 0% -> 0%
where the time goes in v2:
time: 180 us; the launch traced here: 177 us
  Pallas kernels  162 us (90%)
  local copies, waits for them, and re-layouts  8.83 us (5%)
  matrix products  5.03 us (3%)
    pallas_call x1, Pallas kernels, step(): pl.pallas_call(step_kernel, name='step', out_shape=jax.ShapeDtypeStruct((...  162 us
    dot_general x1, local copies, waits for them, and re-layouts, dot(): lax.dot_general(a, b, (((ca,), (cb,)), ((), ())), precision=precision, pr...  5.63 us
    dot_general x1, matrix products, dot(): lax.dot_general(a, b, (((ca,), (cb,)), ((), ())), precision=precision, pr...  5.03 us

profile of v2, /device:TPU:56, one launch (start us, length us, event | category | flops | bytes accessed | tf_op | source)
XLA Modules:
  0.0 176.8 jit_solution(14990608757284158998)
XLA Ops:
  0.7 5.0 %convolution_bitcast_fusion = f32[8192,128]{0,1:T(8,128)} fusion(bf16[256,8192]{1,0:T(8,128)(2,1)} %param.4, bf16[256,128]{1,0:T(8,128)(2,1)} %param.5, pred[256]{0:T(512)(128)(4,1)S(1)} %iota_compare_fusion), kind=kOutput, calls=%fused_computation | convolution fusion | flops 536903680 | bytes 8454400 | tf_op jit(solution)/shard_map/dot_general | solution.py:30
  5.7 0.0 copy-start
  5.7 5.6 %copy.5 = f32[8192,128]{1,0:T(8,128)} copy(f32[8192,128]{0,1:T(8,128)} %convolution_bitcast_fusion) | data formatting | bytes 8388608 | tf_op jit(solution)/shard_map/dot_general | solution.py:30
  11.3 0.0 copy-done
  11.3 0.8 copy.7
  12.2 162.2 %step.1 = f32[32,16,256]{2,1,0:T(8,128)} custom-call(f32[2,8,4,4,2,16,128]{6,5,4,3,2,1,0:T(8,128)} %bitcast.8, f32[32,16,256]{2,1,0:T(8,128)} %bitcast.10), custom_call_target="tpu_custom_call" | custom-call | tf_op jit(solution)/shard_map/step/pallas_call | solution.py:497
  174.4 2.4 %copy.6 = f32[1,512,1,256]{3,2,1,0:T(1,128)} copy(f32[1,512,1,256]{3,1,2,0:T(8,128)} %bitcast.9) | data formatting | bytes 1048576 | tf_op jit(solution)/shard_map/reshape | solution.py:527
  (1 shorter events, 0.0 us)
Async XLA Ops:
  5.7 5.6 %copy-start = (f32[1,512,1,256]{3,2,1,0:T(1,128)S(1)}, f32[1,512,1,256]{3,2,1,0:T(1,128)}, u32[]{:S(2)}) copy-start(f32[1,512,1,256]{3,2,1,0:T(1,128)} %param.7) | copy-start | bytes 1572868

commit v3 on v2

v3 whole, which is shorter than its diff:
```python
import jax
import jax.numpy as jnp
from jax import lax
from jax.sharding import PartitionSpec as P
from jax.experimental import pallas as pl
from jax.experimental.pallas import tpu as pltpu

MESH = pl.DeviceIdType.MESH
HIGH = lax.Precision.HIGHEST
F32, BF16 = jnp.float32, jnp.bfloat16


def position():
    p, q = lax.axis_index("row"), lax.axis_index("col")
    return p, q, p // 8, p % 8, q // 8, (q // 2) % 4, q % 2


def device(zh, y, x, zl, c):
    return (zh * 8 + y, x * 8 + zl * 2 + c)


def send(src, dst, send_sem, recv_sem, target):
    return pltpu.make_async_remote_copy(
        src_ref=src, dst_ref=dst, send_sem=send_sem, recv_sem=recv_sem,
        device_id=target, device_id_type=MESH,
    )


def dot(a, b, ca, cb, precision=None):
    return lax.dot_general(
        a, b, (((ca,), (cb,)), ((), ())), precision=precision, preferred_element_type=F32
    )


def halves(a):
    high = a.astype(BF16)
    return high, (a - high.astype(F32)).astype(BF16)


def dot3(a, b, ca, cb):
    (ah, al), (bh, bl) = halves(a), halves(b)
    return dot(ah, bh, ca, cb) + (dot(ah, bl, ca, cb) + dot(al, bh, ca, cb))


def thirds(a):
    high = a.astype(BF16).astype(F32)
    rest = a - high
    middle = rest.astype(BF16).astype(F32)
    return high, middle, rest - middle


def outer(a, b):
    (ah, am, al), (bh, bm, bl) = thirds(a), thirds(b)
    left = jnp.concatenate([ah, ah, am, am, ah, al], 0).astype(BF16)
    right = jnp.concatenate([bh, bm, bh, bm, bl, bh], 0).astype(BF16)
    return dot(left, right, 0, 0)


def spread_columns(rows, base):
    turned = pltpu.roll(rows, (128 - base) % 128, 1)
    return [jnp.broadcast_to(turned[:, j : j + 1], (8, 128)) for j in range(8)]


def cholesky_block(k, a, ut):
    base = pl.multiple_of(8 * k, 8)
    sub = lax.broadcasted_iota(jnp.int32, (8, 128), 0)
    lane = lax.broadcasted_iota(jnp.int32, (8, 128), 1)
    rows = a[pl.ds(base, 8), :]
    cols = spread_columns(rows, base)
    for j in range(8):
        pivot = cols[j][j : j + 1]
        inv = lax.rsqrt(pivot)
        inv = inv * (1.5 - 0.5 * pivot * inv * inv)
        unit = rows[j : j + 1] * inv
        factor = jnp.where(sub > j, cols[j] * inv, 0.0)
        rows = jnp.where(sub == j, unit, rows - factor * unit)
        for i in range(j + 1, 8):
            cols[i] = cols[i] - factor * (cols[i][j : j + 1] * inv)
    done = jnp.where(lane >= base + sub, rows, 0.0)
    ut[pl.ds(base, 8), :] = done
    a[...] -= outer(done, done)


def inverse_block(k, n, t, lower, upper):
    base = pl.multiple_of(8 * k, 8)
    sub = lax.broadcasted_iota(jnp.int32, (8, 128), 0)
    rows, turned = n[pl.ds(base, 8), :], t[pl.ds(base, 8), :]
    rc, tc = spread_columns(rows[:, :128], base), spread_columns(turned[:, :128], base)
    scale = jnp.zeros((8, 128), F32)
    for j in range(8):
        inv = 1.0 / rc[j][j : j + 1]
        scale = jnp.where(sub == j, inv, scale)
        down = jnp.where(sub > j, rc[j] * inv, 0.0)
        across = jnp.where(sub > j, tc[j] * inv, 0.0)
        rows = rows - jnp.concatenate([down, down], 1) * rows[j : j + 1]
        turned = turned - jnp.concatenate([across, across], 1) * turned[j : j + 1]
        for i in range(j + 1, 8):
            rc[i] = rc[i] - down * rc[i][j : j + 1]
            tc[i] = tc[i] - across * tc[i][j : j + 1]
    turned = turned * jnp.concatenate([scale, scale], 1)
    lower[pl.ds(base, 8), :] = rows[:, 128:]
    upper[pl.ds(base, 8), :] = turned[:, 128:]
    n[...] -= outer(turned[:, :128], rows)
    t[...] -= outer(rows[:, :128], turned)


def step_kernel(psi, hpsi, counts, stored, out, bands, part, theirs, wa, wb, ra1, rb1, a1, b1, ra2,
                rb2, ab2, r3, own, srow, scol, mh, slr, slc, gram, cross, gx, gfull, s1, tops, m1c, m1r,
                raw, rawt, xt, tpart, xin, xown, xr, xc, work, ut, n, t, lower, upper, zr, zc, tx, tfull,
                load, ss, rs, ss_b, rs_b, ss_p, rs_p, ss_r, rs_r, ss_c, rs_c, ss_g, rs_g, ss_h, rs_h,
                ss_s, rs_s, ss_m, rs_m, ss_k, rs_k, ss_x, rs_x, ss_y, rs_y, ss_z, rs_z,
                ss_w, rs_w, ss_v, rs_v):
    p, q, zh, y, x, zl, c = position()
    z = zh * 4 + zl
    first = c == 0
    f = jnp.where(first, y, z)
    s = jnp.where(first, z, y)
    half, slot = q // 16, q % 16
    piece_at = q // 2
    row_slot = 16 * (q % 2) + q // 2
    home = p + 16 * (q % 2)
    at_home = home == q

    def at(xx, ff, sf):
        yy, zz = jnp.where(first, ff, sf), jnp.where(first, sf, ff)
        return device(zz // 4, yy, xx, zz % 4, c)

    def loop(start, stop, body):
        def step(i, carry):
            body(i)
            return carry
        lax.fori_loop(start, stop, step, 0)

    def fetch(g):
        xx = (x + 1 + g) % 4
        return pltpu.make_async_copy(
            psi.at[:, pl.ds(pl.multiple_of(2048 * xx, 2048), 2048)], bands.at[xx], load.at[g]
        )

    for g in range(4):
        fetch(g).start()

    partner = device(zh, y, x, zl, 1 - c)
    barrier = pltpu.get_barrier_semaphore()

    def hail(who):
        pl.semaphore_signal(barrier, inc=1, device_id=who, device_id_type=MESH)

    def hail_unless_me(who):
        @pl.when((who[0] != p) | (who[1] != q))
        def _():
            hail(who)

    hail(partner)
    for d in range(1, 4):
        hail(at((x + d) % 4, f, s))
    for d in range(1, 8):
        hail(at(x, (f + d) % 8, s))
        hail(at(x, f, (s + d) % 8))
    loop(1, 16, lambda d: hail(((p + d) % 16, q)))
    loop(1, 32, lambda d: hail((p, (q + d) % 32)))
    loop(0, 16, lambda j: hail_unless_me((slot, 2 * j + half)))

    live = lax.broadcasted_iota(jnp.int32, (256, 128), 0) < counts[0]
    panel = jnp.where(live, hpsi[...].astype(F32), 0.0).astype(BF16)
    raw[...] = stored[0]
    for h in range(2):
        for j in range(16):
            mh[16 * h + j] = stored[2 * j + h]

    in_rim = (q >= 8) & (q < 16)
    rim = jnp.clip(q - 8, 0, 7) // 2

    @pl.when(in_rim)
    def _():
        for h in range(2):
            rawt[h] = mh[16 * h : 16 * h + 16, :, :128].reshape(256, 128).T[:16]
        m1r[:, rim, c] = rawt[...]


    def multiply(g):
        xx = (x + 1 + g) % 4
        fetch(g).wait()

        def four(i):
            for u in range(4):
                at_chunk = pl.ds(pl.multiple_of(512 * i + 128 * u, 128), 128)
                part[xx, i, u // 2, u % 2] = dot(bands[xx, :, at_chunk], panel, 0, 0).reshape(8, 16, 128)

        loop(0, 4, four)

    def swap(g):
        xx = (x + 1 + g) % 4
        return send(part.at[xx, :, 1 - c], theirs.at[xx], ss_p.at[g], rs_p.at[g], partner)

    for g in range(3):
        multiply(g)
    pl.semaphore_wait(barrier, 18 + 15 + 31 + 15 + jnp.where(at_home, 0, 1))
    for g in range(3):
        swap(g).start()

    from_panel = jnp.maximum(p - 8, 0)

    def put_m(d):
        return send(raw, m1c.at[from_panel], ss_m.at[d], rs_m.at[from_panel], ((p + d) % 16, q))

    def put_k(d):
        return send(rawt, m1r.at[:, rim, c], ss_k.at[d], rs_k.at[rim], (p, (q + 2 * d) % 32))

    @pl.when(in_rim)
    def _():
        loop(1, 16, lambda d: put_k(d).start())

    @pl.when(p >= 8)
    def _():
        m1c[from_panel] = raw[...]
        loop(1, 16, lambda d: put_m(d).start())

    multiply(3)
    swap(3).start()

    def stage_a(g):
        xx = (x + 1 + g) % 4
        return send(wa.at[xx], ra1.at[g], ss.at[g], rs.at[g], at(xx, f, s))

    def stage_b(g, d):
        xx, ff = (x + 1 + g) % 4, (f + d) % 8
        return send(
            wb.at[ff, xx], rb1.at[d - 1, xx], ss_b.at[8 * g + d], rs_b.at[8 * g + d], at(x, ff, s)
        )

    for g in range(4):
        xx = (x + 1 + g) % 4
        swap(g).wait()

        def join(ff):
            for sf in range(8):
                yy, zz = jnp.where(first, ff, sf), jnp.where(first, sf, ff)
                hh, ll = zz // 4, zz % 4
                total = part[xx, ll, c, hh, yy] + theirs[xx, ll, hh, yy]
                wa[xx, ff, sf] = total[:8]
                wb[ff, xx, sf] = total[8:]

        loop(0, 8, join)
        if g < 3:
            stage_a(g).start()
        loop(1, 8, lambda d: stage_b(g, d).start())

    for g in range(4):
        loop(1, 8, lambda d: stage_b(g, d).wait())

    def sum_b1(i):
        total = wb[f, i]
        for d in range(7):
            total += rb1[d, i]
        b1[i] = total

    loop(0, 4, sum_b1)
    copies_b = []
    for d in range(1, 4):
        xx = (x + d) % 4
        copies_b.append(send(b1.at[xx], rb2.at[d - 1], ss.at[10 + d], rs.at[10 + d], at(xx, f, s)))
        copies_b[-1].start()
    for g in range(3):
        stage_a(g).wait()

    def sum_a1(i):
        total = wa[x, i]
        for d in range(3):
            total += ra1[d, i]
        a1[i] = total

    loop(0, 8, sum_a1)
    copies_a = []
    for d in range(1, 8):
        ff = (f + d) % 8
        copies_a.append(send(a1.at[ff], ra2.at[d - 1], ss.at[13 + d], rs.at[13 + d], at(x, ff, s)))
        copies_a[-1].start()
    for copy in copies_b:
        copy.wait()
    ab2[:, 1] = b1[x] + rb2[0] + rb2[1] + rb2[2]
    for copy in copies_a:
        copy.wait()
    total = a1[f]
    for d in range(7):
        total += ra2[d]
    ab2[:, 0] = total
    copies = []
    for d in range(1, 8):
        sf = (s + d) % 8
        copies.append(send(ab2.at[sf], r3.at[d - 1], ss.at[20 + d], rs.at[20 + d], at(x, f, sf)))
        copies[-1].start()
    for copy in copies:
        copy.wait()
    total = ab2[s]
    for d in range(7):
        total += r3[d]
    own[...] = total.reshape(16, 128)
    srow[row_slot] = own[...]

    def to_row_group(src, dst, sem, landed):
        return lambda d: send(src, dst, sem.at[d], landed, ((p + d) % 16, q))

    def to_col_group(src, dst, sem, landed):
        return lambda d: send(src, dst, sem.at[d], landed, (p, (q + d) % 32))

    def start_all(copy, stop):
        loop(1, stop, lambda d: copy(d).start())

    def sent_all(copy, stop):
        loop(1, stop, lambda d: copy(d).wait_send())

    def landed(dst, sem):
        send(dst, dst, ss.at[0], sem, (p, q)).wait_recv()

    put_r = to_col_group(own, srow.at[row_slot], ss_r, rs_r.at[row_slot])

    def put_c(d):
        return send(own, scol.at[q // 2], ss_c.at[d], rs_c.at[q // 2], ((p + d) % 16, home))

    start_all(put_c, 16)
    start_all(put_r, 32)

    @pl.when(at_home)
    def _():
        scol[q // 2] = own[...]

    @pl.when(jnp.logical_not(at_home))
    def _():
        put_c(0).start()

    relay = send(m1r.at[:, :, c], m1r.at[:, :, c], ss.at[28], rs.at[28], partner)

    def take_rim(i):
        @pl.when(8 + 2 * i + c != q)
        def _():
            landed(m1r.at[:, i, c], rs_k.at[i])

    loop(0, 4, take_rim)
    relay.start()

    def take_mc(i):
        @pl.when(i + 8 != p)
        def _():
            landed(m1c.at[i], rs_m.at[i])

    loop(0, 8, take_mc)
    def take_col(buffer, sem):
        def take(j):
            @pl.when((slot != p) | (2 * j + half != q))
            def _():
                landed(buffer.at[j], sem.at[j])

        loop(0, 16, take)

    def take_row(buffer, sem):
        def take(d):
            owner = (q + d) % 32
            at_slot = 16 * (owner % 2) + owner // 2
            landed(buffer.at[at_slot], sem.at[at_slot])

        loop(1, 32, take)

    take_row(srow, rs_r)
    relay.wait_recv()
    zero = jnp.zeros((16, 128), F32)
    slr[...] = srow[...]

    @pl.when(p < 8)
    def _():
        slr[0] = zero

    low = slr[...].reshape(512, 128)
    gram[...] = dot(low, low, 0, 0, HIGH)
    cross[...] = dot3(m1r[0].reshape(128, 256), low[:256], 1, 0) + dot3(
        m1r[1].reshape(128, 256), low[256:], 1, 0
    )
    at_piece = pl.ds(pl.multiple_of(8 * piece_at, 8), 8)
    gx[p, 0] = gram[at_piece, :]
    gx[p, 1] = cross[at_piece, :]
    put_g = to_row_group(gx.at[p], gx.at[p], ss_g, rs_g.at[p])
    start_all(put_g, 16)
    put_s = to_row_group(s1.at[from_panel], s1.at[from_panel], ss_s, rs_s.at[from_panel])

    @pl.when(p >= 8)
    def _():
        s1[from_panel, 0] = srow[0]
        s1[from_panel, 1] = m1r[0].reshape(128, 256)[:, :128].T[:16]
        start_all(put_s, 16)

    lane = lax.broadcasted_iota(jnp.int32, (16, 128), 1)
    in_left = (lane < 16) & (q < 8)

    @pl.when(q < 8)
    def _():
        left = pltpu.roll(srow[...].reshape(512, 128), (128 - 16 * (q % 8)) % 128, 1).reshape(32, 16, 128)
        mh[:, :, :128] = jnp.where(in_left[None], left, mh[:, :, :128])

    take_col(scol, rs_c)
    slc[...] = scol[...]

    @pl.when(q < 8)
    def _():
        slc[0] = zero

    @pl.when(p < 8)
    def _():
        turned = pltpu.roll(scol[...].reshape(256, 128), (128 - 16 * (p % 8)) % 128, 1)
        upper_rows = turned.T[:16]
        mh[0, :, :128] = jnp.where(
            in_left, 0.5 * (mh[0, :, :128] + upper_rows[:, :128]), upper_rows[:, :128]
        )
        mh[0, :, 128:] = upper_rows[:, 128:]

    xpart = dot3(mh[...].reshape(512, 256), slc[...].reshape(256, 128), 1, 0)
    xt[:, :16] = xpart.reshape(32, 16, 128)
    tpart[...] = dot3(low, xpart, 0, 0)

    def spread(i):
        xt[i, 16:] = tpart[pl.ds(pl.multiple_of(8 * (i % 16), 8), 8), :]

    loop(0, 32, spread)

    def put_x(d):
        to = (q + d) % 32
        return send(
            xt.at[16 * (to % 2) + to // 2], xin.at[q], ss_x.at[d], rs_x.at[q], (p, to)
        )

    start_all(put_x, 32)

    def all_landed(buffer, sem, count, me):
        loop(1, count, lambda d: landed(buffer.at[(me + d) % count], sem.at[(me + d) % count]))

    def total_of(buffer, count):
        total = buffer[0]
        for i in range(1, count):
            total += buffer[i]
        return total

    def put_piece(full, sem, got):
        def copy(d):
            to = (piece_at + d) % 16
            return send(full.at[piece_at], full.at[piece_at], sem.at[d], got.at[piece_at], (p, 2 * to + c))
        return copy

    all_landed(gx, rs_g, 16, p)
    gfull[piece_at] = total_of(gx, 16)
    put_h = put_piece(gfull, ss_h, rs_h)
    start_all(put_h, 16)

    all_landed(xin, rs_x, 32, q)
    xin[q] = xt[row_slot]
    both = total_of(xin, 32)
    xown[...] = both[:16]
    tx[p] = both[16:]
    xr[row_slot] = both[:16]
    put_w = to_row_group(tx.at[p], tx.at[p], ss_w, rs_w.at[p])
    start_all(put_w, 16)
    put_y = to_col_group(xown, xr.at[row_slot], ss_y, rs_y.at[row_slot])
    start_all(put_y, 32)

    def put_z(d):
        return send(xown, xc.at[q // 2], ss_z.at[d], rs_z.at[q // 2], ((p + d) % 16, home))

    start_all(put_z, 16)

    @pl.when(at_home)
    def _():
        xc[q // 2] = xown[...]

    @pl.when(jnp.logical_not(at_home))
    def _():
        put_z(0).start()

    all_landed(gfull, rs_h, 16, piece_at)
    gram_all = gfull[:, 0].reshape(128, 128)
    work[...] = gram_all
    loop(0, 16, lambda k: cholesky_block(k, work, ut))

    def take_from_panel(i):
        @pl.when(i + 8 != p)
        def _():
            landed(s1.at[i], rs_s.at[i])

    loop(0, 8, take_from_panel)
    tops[...] = s1[:, 0].reshape(128, 128)
    normal = gram_all - dot(ut[...], tops[...], 0, 0, HIGH)
    eye = (
        lax.broadcasted_iota(jnp.int32, (128, 128), 0) == lax.broadcasted_iota(jnp.int32, (128, 128), 1)
    ).astype(F32)
    n[:, :128] = normal
    n[:, 128:] = eye
    t[:, :128] = normal.T
    t[:, 128:] = eye
    all_landed(tx, rs_w, 16, p)
    tfull[piece_at] = total_of(tx, 16)
    put_v = put_piece(tfull, ss_v, rs_v)
    start_all(put_v, 16)
    loop(0, 16, lambda k: inverse_block(k, n, t, lower, upper))
    inverse_t = dot(lower[...], upper[...], 0, 0, HIGH)
    work[...] = inverse_t
    root = ut[...]
    turn = dot(gfull[:, 1].reshape(128, 128), root, 0, 0, HIGH)
    rest = dot(dot(root, s1[:, 1].reshape(128, 128), 0, 0, HIGH), root, 1, 0, HIGH) - (turn + turn.T)

    @pl.when(p >= 8)
    def _():
        slr[0] -= ut[pl.ds(pl.multiple_of(16 * from_panel, 16), 16), :]

    @pl.when((q >= 8) & (q < 16))
    def _():
        slc[0] -= ut[pl.ds(pl.multiple_of(16 * jnp.clip(q - 8, 0, 7), 16), 16), :]

    all_lanes = lax.broadcasted_iota(jnp.int32, (128, 128), 1)

    def patched(block, at_tile):
        fresh = pltpu.roll(tops[...], (128 - 16 * (at_tile % 8)) % 128, 1)
        return jnp.where((all_lanes < 16) & (at_tile < 8), fresh, block)

    rim0 = m1r[0].reshape(128, 256)
    rim0 = jnp.concatenate([patched(rim0[:, :128], p), rim0[:, 128:]], 1)
    rimc = m1c[...].reshape(128, 256)
    rimc = jnp.concatenate([patched(rimc[:, :128], q), rimc[:, 128:]], 1)
    zr[...] = jnp.concatenate(
        [dot3(rim0, root, 0, 0), dot3(m1r[1].reshape(128, 256), root, 0, 0)], 0
    )
    zc[...] = dot3(rimc, root, 0, 0)
    take_row(xr, rs_y)
    take_col(xc, rs_z)
    acols = dot3(xc[...].reshape(256, 128) - zc[...], work[...], 1, 0)
    ycols = slc[...].reshape(256, 128)
    rh, rl = halves(jnp.concatenate([acols, ycols], 1))
    for h in range(4):
        rows = slr[pl.ds(8 * h, 8)].reshape(128, 128)
        brows = dot3(
            xr[pl.ds(8 * h, 8)].reshape(128, 128) - zr[pl.ds(128 * h, 128), :], work[...], 1, 0
        )
        lh, ll = halves(jnp.concatenate([rows, brows], 1))
        change = dot(lh, rh, 1, 1) + (dot(lh, rl, 1, 1) + dot(ll, rh, 1, 1))
        mh[pl.ds(8 * h, 8)] = mh[pl.ds(8 * h, 8)] - change.reshape(8, 16, 256)
    all_landed(tfull, rs_v, 16, piece_at)
    wmat = tfull[...].reshape(128, 128) + rest
    core = dot(dot(work[...], wmat, 0, 0, HIGH), work[...], 1, 0, HIGH)
    ch, cl = halves(dot3(ycols, core, 1, 1))
    for h in range(4):
        lh, ll = halves(slr[pl.ds(8 * h, 8)].reshape(128, 128))
        change = dot(lh, ch, 1, 1) + (dot(lh, cl, 1, 1) + dot(ll, ch, 1, 1))
        for i in range(8):
            at_tile = 8 * h + i
            out[2 * (at_tile % 16) + at_tile // 16] = mh[at_tile] + change[16 * i : 16 * i + 16]

    sent_all(put_c, 16)
    sent_all(put_r, 32)
    sent_all(put_g, 16)
    sent_all(put_h, 16)
    sent_all(put_x, 32)
    sent_all(put_y, 32)
    sent_all(put_z, 16)
    sent_all(put_w, 16)
    sent_all(put_v, 16)

    relay.wait_send()

    @pl.when(jnp.logical_not(at_home))
    def _():
        put_c(0).wait_send()
        put_z(0).wait_send()

    @pl.when(p >= 8)
    def _():
        sent_all(put_s, 16)
        sent_all(put_m, 16)

    @pl.when(in_rim)
    def _():
        sent_all(put_k, 16)


def step(psi, hpsi, counts, stored):
    vmem = pl.BlockSpec(memory_space=pltpu.VMEM)

    def room(*dims):
        return pltpu.VMEM(dims, F32)

    sems = [4, 32, 32, 32, 32, 4, 4, 32, 32, 16, 16, 16, 16, 16, 16, 16, 8, 16, 8, 16, 16, 32, 32, 32, 32, 16, 16, 16, 16, 16, 16]
    return pl.pallas_call(
        step_kernel,
        name="step",
        out_shape=jax.ShapeDtypeStruct((32, 16, 256), F32),
        in_specs=[pl.BlockSpec(memory_space=pltpu.HBM), vmem, pl.BlockSpec(memory_space=pltpu.SMEM), vmem],
        out_specs=vmem,
        scratch_shapes=[
            pltpu.VMEM((4, 256, 2048), BF16), room(4, 4, 2, 2, 8, 16, 128),
            room(4, 4, 2, 8, 16, 128), room(4, 8, 8, 8, 128), room(8, 4, 8, 8, 128),
            room(3, 8, 8, 8, 128), room(7, 4, 8, 8, 128), room(8, 8, 8, 128), room(4, 8, 8, 128),
            room(7, 8, 8, 128), room(3, 8, 8, 128), room(8, 2, 8, 128), room(7, 2, 8, 128),
            room(16, 128),
            room(32, 16, 128), room(16, 16, 128), room(32, 16, 256), room(32, 16, 128),
            room(16, 16, 128), room(128, 128), room(128, 128), room(16, 2, 8, 128),
            room(16, 2, 8, 128), room(8, 2, 16, 128), room(128, 128), room(8, 16, 256),
            room(2, 4, 2, 16, 256), room(16, 256), room(2, 16, 256), room(32, 24, 128), room(128, 128),
            room(32, 24, 128), room(16, 128), room(32, 16, 128), room(16, 16, 128),
            room(128, 128), room(128, 128), room(128, 256), room(128, 256), room(128, 128),
            room(128, 128), room(512, 128), room(256, 128), room(16, 8, 128), room(16, 8, 128),
        ] + [pltpu.SemaphoreType.DMA((k,)) for k in sems],
        compiler_params=pltpu.CompilerParams(
            collective_id=1, has_side_effects=True, vmem_limit_bytes=62 << 20
        ),
    )(psi, hpsi, counts, stored)


def per_device(psi, hpsi, slab_counts, matrix):
    return step(psi, hpsi, slab_counts, matrix.reshape(32, 16, 256)).reshape(matrix.shape)


def solution(mesh):
    in_specs = (
        P(("row", "col"), None),
        P(("row", "col"), None),
        P(("row", "col")),
        P("row", None, "col", None),
    )
    out_specs = P("row", None, "col", None)
    return jax.shard_map(
        per_device, mesh=mesh, in_specs=in_specs, out_specs=out_specs, check_vma=False
    )
```

time: 180 us -> 121 us (0.67); the launches traced: 177 us -> 121 us
  Pallas kernels: 162 us -> 116 us
  matrix products: 5.03 us -> 0 us
  local copies, waits for them, and re-layouts: 8.83 us -> 4.24 us
    pallas_call x1, Pallas kernels: 162 us -> 116 us  [step(): pl.pallas_call(step_kernel, name='step', out_shape=jax.ShapeDtypeStruct((...]
    dot_general x1 -> x0, local copies, waits for them, and re-layouts: 5.63 us -> none  [dot(): lax.dot_general(a, b, (((ca,), (cb,)), ((), ())), precision=precision, pr...]
    dot_general x1 -> x0, matrix products: 5.03 us -> none  [dot(): lax.dot_general(a, b, (((ca,), (cb,)), ((), ())), precision=precision, pr...]
where the time goes in v3:
time: 121 us
  Pallas kernels  116 us (96%)
  local copies, waits for them, and re-layouts  4.24 us (4%)
    pallas_call x1, Pallas kernels, step(): pl.pallas_call(step_kernel, name='step', out_shape=jax.ShapeDtypeStruct((...  116 us

profile of v3, /device:TPU:56, one launch (start us, length us, event | category | flops | bytes accessed | tf_op | source)
XLA Modules:
  0.0 120.8 jit_solution(13170364089277079406)
XLA Ops:
  0.7 1.9 %copy.6 = f32[1,512,1,256]{3,1,2,0:T(8,128)} copy(f32[1,512,1,256]{3,2,1,0:T(1,128)} %param.7) | data formatting | bytes 1048576
  2.5 115.9 %step.1 = f32[32,16,256]{2,1,0:T(8,128)} custom-call(bf16[256,8192]{1,0:T(8,128)(2,1)} %psi.1, bf16[256,128]{1,0:T(8,128)(2,1)} %hpsi.1, s32[1]{0:T(128)S(6)} %copy.7.counts, f32[32,16,256]{2,1,0:T(8,128)} %bitcast.3), custom_call_target="tpu_custom_call" | custom-call | tf_op jit(solution)/shard_map/step/pallas_call | solution.py:587
  118.4 2.4 %copy.5 = f32[1,512,1,256]{3,2,1,0:T(1,128)} copy(f32[1,512,1,256]{3,1,2,0:T(8,128)} %bitcast.2) | data formatting | bytes 1048576 | tf_op jit(solution)/shard_map/reshape | solution.py:614

commit v4 on v3

--- a/solution.py
+++ b/solution.py
@@ -7,6 +7,7 @@
 
 MESH = pl.DeviceIdType.MESH
 HIGH = lax.Precision.HIGHEST
+BLOCK = 16
 F32, BF16 = jnp.float32, jnp.bfloat16
 
 
@@ -58,55 +59,55 @@
 
 def spread_columns(rows, base):
     turned = pltpu.roll(rows, (128 - base) % 128, 1)
-    return [jnp.broadcast_to(turned[:, j : j + 1], (8, 128)) for j in range(8)]
+    return [jnp.broadcast_to(turned[:, j : j + 1], (BLOCK, 128)) for j in range(BLOCK)]
 
 
 def cholesky_block(k, a, ut):
-    base = pl.multiple_of(8 * k, 8)
-    sub = lax.broadcasted_iota(jnp.int32, (8, 128), 0)
-    lane = lax.broadcasted_iota(jnp.int32, (8, 128), 1)
-    rows = a[pl.ds(base, 8), :]
+    base = pl.multiple_of(BLOCK * k, BLOCK)
+    sub = lax.broadcasted_iota(jnp.int32, (BLOCK, 128), 0)
+    lane = lax.broadcasted_iota(jnp.int32, (BLOCK, 128), 1)
+    rows = a[pl.ds(base, BLOCK), :]
     cols = spread_columns(rows, base)
-    for j in range(8):
+    for j in range(BLOCK):
         pivot = cols[j][j : j + 1]
         inv = lax.rsqrt(pivot)
         inv = inv * (1.5 - 0.5 * pivot * inv * inv)
         unit = rows[j : j + 1] * inv
         factor = jnp.where(sub > j, cols[j] * inv, 0.0)
         rows = jnp.where(sub == j, unit, rows - factor * unit)
-        for i in range(j + 1, 8):
+        for i in range(j + 1, BLOCK):
             cols[i] = cols[i] - factor * (cols[i][j : j + 1] * inv)
     done = jnp.where(lane >= base + sub, rows, 0.0)
-    ut[pl.ds(base, 8), :] = done
+    ut[pl.ds(base, BLOCK), :] = done
     a[...] -= outer(done, done)
 
 
 def inverse_block(k, n, t, lower, upper):
-    base = pl.multiple_of(8 * k, 8)
-    sub = lax.broadcasted_iota(jnp.int32, (8, 128), 0)
-    rows, turned = n[pl.ds(base, 8), :], t[pl.ds(base, 8), :]
+    base = pl.multiple_of(BLOCK * k, BLOCK)
+    sub = lax.broadcasted_iota(jnp.int32, (BLOCK, 128), 0)
+    rows, turned = n[pl.ds(base, BLOCK), :], t[pl.ds(base, BLOCK), :]
     rc, tc = spread_columns(rows[:, :128], base), spread_columns(turned[:, :128], base)
-    scale = jnp.zeros((8, 128), F32)
-    for j in range(8):
+    scale = jnp.zeros((BLOCK, 128), F32)
+    for j in range(BLOCK):
         inv = 1.0 / rc[j][j : j + 1]
         scale = jnp.where(sub == j, inv, scale)
         down = jnp.where(sub > j, rc[j] * inv, 0.0)
         across = jnp.where(sub > j, tc[j] * inv, 0.0)
         rows = rows - jnp.concatenate([down, down], 1) * rows[j : j + 1]
         turned = turned - jnp.concatenate([across, across], 1) * turned[j : j + 1]
-        for i in range(j + 1, 8):
+        for i in range(j + 1, BLOCK):
             rc[i] = rc[i] - down * rc[i][j : j + 1]
             tc[i] = tc[i] - across * tc[i][j : j + 1]
     turned = turned * jnp.concatenate([scale, scale], 1)
-    lower[pl.ds(base, 8), :] = rows[:, 128:]
-    upper[pl.ds(base, 8), :] = turned[:, 128:]
+    lower[pl.ds(base, BLOCK), :] = rows[:, 128:]
+    upper[pl.ds(base, BLOCK), :] = turned[:, 128:]
     n[...] -= outer(turned[:, :128], rows)
     t[...] -= outer(rows[:, :128], turned)
 
 
 def step_kernel(psi, hpsi, counts, stored, out, bands, part, theirs, wa, wb, ra1, rb1, a1, b1, ra2,
                 rb2, ab2, r3, own, srow, scol, mh, slr, slc, gram, cross, gx, gfull, s1, tops, m1c, m1r,
-                raw, rawt, xt, tpart, xin, xown, xr, xc, work, ut, n, t, lower, upper, zr, zc, tx, tfull,
+                raw, rawt, xt, xo, xsum, tpart, xin, xown, xr, xc, work, ut, n, t, lower, upper, zr, zc, tx, tfull,
                 load, ss, rs, ss_b, rs_b, ss_p, rs_p, ss_r, rs_r, ss_c, rs_c, ss_g, rs_g, ss_h, rs_h,
                 ss_s, rs_s, ss_m, rs_m, ss_k, rs_k, ss_x, rs_x, ss_y, rs_y, ss_z, rs_z,
                 ss_w, rs_w, ss_v, rs_v):
@@ -163,11 +164,15 @@
 
     live = lax.broadcasted_iota(jnp.int32, (256, 128), 0) < counts[0]
     panel = jnp.where(live, hpsi[...].astype(F32), 0.0).astype(BF16)
-    raw[...] = stored[0]
+    def halves_of(i):
+        return [pl.ds(32 * i + k, 16, stride=2) for k in range(2)]
+
     for h in range(2):
         for j in range(16):
-            mh[16 * h + j] = stored[2 * j + h]
-
+            for k, lines in enumerate(halves_of(2 * j + h)):
+                mh[16 * h + j, :, 128 * k : 128 * k + 128] = stored[lines, :]
+
+    raw[...] = mh[0]
     in_rim = (q >= 8) & (q < 16)
     rim = jnp.clip(q - 8, 0, 7) // 2
 
@@ -413,21 +418,35 @@
         mh[0, :, 128:] = upper_rows[:, 128:]
 
     xpart = dot3(mh[...].reshape(512, 256), slc[...].reshape(256, 128), 1, 0)
-    xt[:, :16] = xpart.reshape(32, 16, 128)
+    xt[:, :, :16] = xpart.reshape(2, 16, 16, 128)
     tpart[...] = dot3(low, xpart, 0, 0)
-
-    def spread(i):
-        xt[i, 16:] = tpart[pl.ds(pl.multiple_of(8 * (i % 16), 8), 8), :]
-
-    loop(0, 32, spread)
+    for h in range(2):
+        xt[h, :, 16:] = tpart[...].reshape(16, 8, 128)
+    pair = send(xt.at[1 - c], xo, ss.at[29], rs.at[29], partner)
+    pair.start()
+    pair.wait()
+    xsum[...] = xt[c] + xo[...]
 
     def put_x(d):
-        to = (q + d) % 32
-        return send(
-            xt.at[16 * (to % 2) + to // 2], xin.at[q], ss_x.at[d], rs_x.at[q], (p, to)
-        )
-
-    start_all(put_x, 32)
+        to = (piece_at + d) % 16
+        return send(xsum.at[to], xin.at[piece_at], ss_x.at[d], rs_x.at[piece_at], (p, 2 * to + c))
+
+    start_all(put_x, 16)
+
+    sent_all(put_r, 32)
+    sent_all(put_c, 16)
+
+    @pl.when(jnp.logical_not(at_home))
+    def _():
+        put_c(0).wait_send()
+
+    @pl.when(p >= 8)
+    def _():
+        sent_all(put_m, 16)
+
+    @pl.when(in_rim)
+    def _():
+        sent_all(put_k, 16)
 
     def all_landed(buffer, sem, count, me):
         loop(1, count, lambda d: landed(buffer.at[(me + d) % count], sem.at[(me + d) % count]))
@@ -449,9 +468,9 @@
     put_h = put_piece(gfull, ss_h, rs_h)
     start_all(put_h, 16)
 
-    all_landed(xin, rs_x, 32, q)
-    xin[q] = xt[row_slot]
-    both = total_of(xin, 32)
+    all_landed(xin, rs_x, 16, piece_at)
+    xin[piece_at] = xsum[piece_at]
+    both = total_of(xin, 16)
     xown[...] = both[:16]
     tx[p] = both[16:]
     xr[row_slot] = both[:16]
@@ -473,10 +492,17 @@
     def _():
         put_z(0).start()
 
+    sent_all(put_g, 16)
+    sent_all(put_x, 16)
+
+    @pl.when(p >= 8)
+    def _():
+        sent_all(put_s, 16)
+
     all_landed(gfull, rs_h, 16, piece_at)
     gram_all = gfull[:, 0].reshape(128, 128)
     work[...] = gram_all
-    loop(0, 16, lambda k: cholesky_block(k, work, ut))
+    loop(0, 128 // BLOCK, lambda k: cholesky_block(k, work, ut))
 
     def take_from_panel(i):
         @pl.when(i + 8 != p)
@@ -493,11 +519,12 @@
     n[:, 128:] = eye
     t[:, :128] = normal.T
     t[:, 128:] = eye
+    loop(0, 3, lambda k: inverse_block(k, n, t, lower, upper))
     all_landed(tx, rs_w, 16, p)
     tfull[piece_at] = total_of(tx, 16)
     put_v = put_piece(tfull, ss_v, rs_v)
     start_all(put_v, 16)
-    loop(0, 16, lambda k: inverse_block(k, n, t, lower, upper))
+    loop(3, 128 // BLOCK, lambda k: inverse_block(k, n, t, lower, upper))
     inverse_t = dot(lower[...], upper[...], 0, 0, HIGH)
     work[...] = inverse_t
     root = ut[...]
@@ -539,6 +566,15 @@
         lh, ll = halves(jnp.concatenate([rows, brows], 1))
         change = dot(lh, rh, 1, 1) + (dot(lh, rl, 1, 1) + dot(ll, rh, 1, 1))
         mh[pl.ds(8 * h, 8)] = mh[pl.ds(8 * h, 8)] - change.reshape(8, 16, 256)
+    sent_all(put_h, 16)
+    sent_all(put_y, 32)
+    sent_all(put_z, 16)
+    sent_all(put_w, 16)
+
+    @pl.when(jnp.logical_not(at_home))
+    def _():
+        put_z(0).wait_send()
+
     all_landed(tfull, rs_v, 16, piece_at)
     wmat = tfull[...].reshape(128, 128) + rest
     core = dot(dot(work[...], wmat, 0, 0, HIGH), work[...], 1, 0, HIGH)
@@ -548,33 +584,12 @@
         change = dot(lh, ch, 1, 1) + (dot(lh, cl, 1, 1) + dot(ll, ch, 1, 1))
         for i in range(8):
             at_tile = 8 * h + i
-            out[2 * (at_tile % 16) + at_tile // 16] = mh[at_tile] + change[16 * i : 16 * i + 16]
-
-    sent_all(put_c, 16)
-    sent_all(put_r, 32)
-    sent_all(put_g, 16)
-    sent_all(put_h, 16)
-    sent_all(put_x, 32)
-    sent_all(put_y, 32)
-    sent_all(put_z, 16)
-    sent_all(put_w, 16)
+            tile = mh[at_tile] + change[16 * i : 16 * i + 16]
+            for k, lines in enumerate(halves_of(2 * (at_tile % 16) + at_tile // 16)):
+                out[lines, :] = tile[:, 128 * k : 128 * k + 128]
+
     sent_all(put_v, 16)
-
     relay.wait_send()
-
-    @pl.when(jnp.logical_not(at_home))
-    def _():
-        put_c(0).wait_send()
-        put_z(0).wait_send()
-
-    @pl.when(p >= 8)
-    def _():
-        sent_all(put_s, 16)
-        sent_all(put_m, 16)
-
-    @pl.when(in_rim)
-    def _():
-        sent_all(put_k, 16)
 
 
 def step(psi, hpsi, counts, stored):
@@ -587,7 +602,7 @@
     return pl.pallas_call(
         step_kernel,
         name="step",
-        out_shape=jax.ShapeDtypeStruct((32, 16, 256), F32),
+        out_shape=jax.ShapeDtypeStruct((1024, 128), F32),
         in_specs=[pl.BlockSpec(memory_space=pltpu.HBM), vmem, pl.BlockSpec(memory_space=pltpu.SMEM), vmem],
         out_specs=vmem,
         scratch_shapes=[
@@ -599,8 +614,8 @@
             room(32, 16, 128), room(16, 16, 128), room(32, 16, 256), room(32, 16, 128),
             room(16, 16, 128), room(128, 128), room(128, 128), room(16, 2, 8, 128),
             room(16, 2, 8, 128), room(8, 2, 16, 128), room(128, 128), room(8, 16, 256),
-            room(2, 4, 2, 16, 256), room(16, 256), room(2, 16, 256), room(32, 24, 128), room(128, 128),
-            room(32, 24, 128), room(16, 128), room(32, 16, 128), room(16, 16, 128),
+            room(2, 4, 2, 16, 256), room(16, 256), room(2, 16, 256), room(2, 16, 24, 128), room(16, 24, 128), room(16, 24, 128), room(128, 128),
+            room(16, 24, 128), room(16, 128), room(32, 16, 128), room(16, 16, 128),
             room(128, 128), room(128, 128), room(128, 256), room(128, 256), room(128, 128),
             room(128, 128), room(512, 128), room(256, 128), room(16, 8, 128), room(16, 8, 128),
         ] + [pltpu.SemaphoreType.DMA((k,)) for k in sems],
@@ -611,7 +626,7 @@
 
 
 def per_device(psi, hpsi, slab_counts, matrix):
-    return step(psi, hpsi, slab_counts, matrix.reshape(32, 16, 256)).reshape(matrix.shape)
+    return step(psi, hpsi, slab_counts, matrix.reshape(1024, 128)).reshape(matrix.shape)
 
 
 def solution(mesh):

time: 121 us -> 111 us (0.917); the launches traced: 121 us -> 110 us
  Pallas kernels: 116 us -> 107 us
  local copies, waits for them, and re-layouts: 4.24 us -> 2.19 us
    pallas_call x1, Pallas kernels: 116 us -> 107 us  [step(): pl.pallas_call(step_kernel, name='step', out_shape=jax.ShapeDtypeStruct((...]
    reshape x1 -> x0, local copies, waits for them, and re-layouts: 2.37 us -> none  [per_device(): step(psi, hpsi, slab_counts, matrix.reshape(32, 16, 256))]
where the time goes in v4:
time: 111 us; the launch traced here: 110 us
  Pallas kernels  107 us (96%)
  local copies, waits for them, and re-layouts  2.19 us (2%)
    pallas_call x1, Pallas kernels, step(): pl.pallas_call(step_kernel, name='step', out_shape=jax.ShapeDtypeStruct((...  107 us

profile of v4, /device:TPU:56, one launch (start us, length us, event | category | flops | bytes accessed | tf_op | source)
XLA Modules:
  0.0 109.5 jit_solution(15147935669571470683)
XLA Ops:
  0.7 106.7 %step.1 = f32[1024,128]{1,0:T(8,128)} custom-call(bf16[256,8192]{1,0:T(8,128)(2,1)} %psi.1, bf16[256,128]{1,0:T(8,128)(2,1)} %hpsi.1, s32[1]{0:T(128)S(6)} %copy.7.counts, f32[1024,128]{1,0:T(8,128)} %bitcast.3), custom_call_target="tpu_custom_call" | custom-call | tf_op jit(solution)/shard_map/step/pallas_call | solution.py:602
  107.3 2.2 %copy.8 = f32[1,512,1,256]{3,2,1,0:T(1,128)} copy(f32[1,512,1,256]{3,2,1,0:T(1,128)} %bitcast.2) | data formatting | bytes 1048576

commit v5 on v4

--- a/solution.py
+++ b/solution.py
@@ -105,7 +105,7 @@
     t[...] -= outer(rows[:, :128], turned)
 
 
-def step_kernel(psi, hpsi, counts, stored, out, bands, part, theirs, wa, wb, ra1, rb1, a1, b1, ra2,
+def step_kernel(psi, hpsi_far, counts, stored_far, out, hpsi, stored, bands, part, theirs, wa, wb, ra1, rb1, a1, b1, ra2,
                 rb2, ab2, r3, own, srow, scol, mh, slr, slc, gram, cross, gx, gfull, s1, tops, m1c, m1r,
                 raw, rawt, xt, xo, xsum, tpart, xin, xown, xr, xc, work, ut, n, t, lower, upper, zr, zc, tx, tfull,
                 load, ss, rs, ss_b, rs_b, ss_p, rs_p, ss_r, rs_r, ss_c, rs_c, ss_g, rs_g, ss_h, rs_h,
@@ -138,8 +138,12 @@
             psi.at[:, pl.ds(pl.multiple_of(2048 * xx, 2048), 2048)], bands.at[xx], load.at[g]
         )
 
+    fetch_panel = pltpu.make_async_copy(hpsi_far, hpsi, load.at[4])
+    fetch_matrix = pltpu.make_async_copy(stored_far, stored, load.at[5])
+    fetch_panel.start()
     for g in range(4):
         fetch(g).start()
+    fetch_matrix.start()
 
     partner = device(zh, y, x, zl, 1 - c)
     barrier = pltpu.get_barrier_semaphore()
@@ -162,8 +166,28 @@
     loop(1, 32, lambda d: hail((p, (q + d) % 32)))
     loop(0, 16, lambda j: hail_unless_me((slot, 2 * j + half)))
 
+    fetch_panel.wait()
     live = lax.broadcasted_iota(jnp.int32, (256, 128), 0) < counts[0]
     panel = jnp.where(live, hpsi[...].astype(F32), 0.0).astype(BF16)
+    def multiply(g):
+        xx = (x + 1 + g) % 4
+        fetch(g).wait()
+
+        def four(i):
+            for u in range(4):
+                at_chunk = pl.ds(pl.multiple_of(512 * i + 128 * u, 128), 128)
+                part[xx, i, u // 2, u % 2] = dot(bands[xx, :, at_chunk], panel, 0, 0).reshape(8, 16, 128)
+
+        loop(0, 4, four)
+
+    def swap(g):
+        xx = (x + 1 + g) % 4
+        return send(part.at[xx, :, 1 - c], theirs.at[xx], ss_p.at[g], rs_p.at[g], partner)
+
+    for g in range(4):
+        multiply(g)
+    fetch_matrix.wait()
+
     def halves_of(i):
         return [pl.ds(32 * i + k, 16, stride=2) for k in range(2)]
 
@@ -183,25 +207,8 @@
         m1r[:, rim, c] = rawt[...]
 
 
-    def multiply(g):
-        xx = (x + 1 + g) % 4
-        fetch(g).wait()
-
-        def four(i):
-            for u in range(4):
-                at_chunk = pl.ds(pl.multiple_of(512 * i + 128 * u, 128), 128)
-                part[xx, i, u // 2, u % 2] = dot(bands[xx, :, at_chunk], panel, 0, 0).reshape(8, 16, 128)
-
-        loop(0, 4, four)
-
-    def swap(g):
-        xx = (x + 1 + g) % 4
-        return send(part.at[xx, :, 1 - c], theirs.at[xx], ss_p.at[g], rs_p.at[g], partner)
-
-    for g in range(3):
-        multiply(g)
     pl.semaphore_wait(barrier, 18 + 15 + 31 + 15 + jnp.where(at_home, 0, 1))
-    for g in range(3):
+    for g in range(4):
         swap(g).start()
 
     from_panel = jnp.maximum(p - 8, 0)
@@ -215,14 +222,6 @@
     @pl.when(in_rim)
     def _():
         loop(1, 16, lambda d: put_k(d).start())
-
-    @pl.when(p >= 8)
-    def _():
-        m1c[from_panel] = raw[...]
-        loop(1, 16, lambda d: put_m(d).start())
-
-    multiply(3)
-    swap(3).start()
 
     def stage_a(g):
         xx = (x + 1 + g) % 4
@@ -281,6 +280,12 @@
         ff = (f + d) % 8
         copies_a.append(send(a1.at[ff], ra2.at[d - 1], ss.at[13 + d], rs.at[13 + d], at(x, ff, s)))
         copies_a[-1].start()
+
+    @pl.when(p >= 8)
+    def _():
+        m1c[from_panel] = raw[...]
+        loop(1, 16, lambda d: put_m(d).start())
+
     for copy in copies_b:
         copy.wait()
     ab2[:, 1] = b1[x] + rb2[0] + rb2[1] + rb2[2]
@@ -323,8 +328,8 @@
     def put_c(d):
         return send(own, scol.at[q // 2], ss_c.at[d], rs_c.at[q // 2], ((p + d) % 16, home))
 
+    start_all(put_r, 32)
     start_all(put_c, 16)
-    start_all(put_r, 32)
 
     @pl.when(at_home)
     def _():
@@ -349,7 +354,6 @@
         def _():
             landed(m1c.at[i], rs_m.at[i])
 
-    loop(0, 8, take_mc)
     def take_col(buffer, sem):
         def take(j):
             @pl.when((slot != p) | (2 * j + half != q))
@@ -367,7 +371,6 @@
         loop(1, 32, take)
 
     take_row(srow, rs_r)
-    relay.wait_recv()
     zero = jnp.zeros((16, 128), F32)
     slr[...] = srow[...]
 
@@ -377,21 +380,11 @@
 
     low = slr[...].reshape(512, 128)
     gram[...] = dot(low, low, 0, 0, HIGH)
-    cross[...] = dot3(m1r[0].reshape(128, 256), low[:256], 1, 0) + dot3(
-        m1r[1].reshape(128, 256), low[256:], 1, 0
-    )
     at_piece = pl.ds(pl.multiple_of(8 * piece_at, 8), 8)
-    gx[p, 0] = gram[at_piece, :]
-    gx[p, 1] = cross[at_piece, :]
+    gx[p] = gram[at_piece, :]
     put_g = to_row_group(gx.at[p], gx.at[p], ss_g, rs_g.at[p])
     start_all(put_g, 16)
     put_s = to_row_group(s1.at[from_panel], s1.at[from_panel], ss_s, rs_s.at[from_panel])
-
-    @pl.when(p >= 8)
-    def _():
-        s1[from_panel, 0] = srow[0]
-        s1[from_panel, 1] = m1r[0].reshape(128, 256)[:, :128].T[:16]
-        start_all(put_s, 16)
 
     lane = lax.broadcasted_iota(jnp.int32, (16, 128), 1)
     in_left = (lane < 16) & (q < 8)
@@ -432,7 +425,17 @@
         return send(xsum.at[to], xin.at[piece_at], ss_x.at[d], rs_x.at[piece_at], (p, 2 * to + c))
 
     start_all(put_x, 16)
-
+    relay.wait_recv()
+    cross[...] = dot3(m1r[0].reshape(128, 256), low[:256], 1, 0) + dot3(
+        m1r[1].reshape(128, 256), low[256:], 1, 0
+    )
+    @pl.when(p >= 8)
+    def _():
+        s1[from_panel, 0] = srow[0]
+        s1[from_panel, 1] = m1r[0].reshape(128, 256)[:, :128].T[:16]
+        start_all(put_s, 16)
+
+    loop(0, 8, take_mc)
     sent_all(put_r, 32)
     sent_all(put_c, 16)
 
@@ -472,7 +475,8 @@
     xin[piece_at] = xsum[piece_at]
     both = total_of(xin, 16)
     xown[...] = both[:16]
-    tx[p] = both[16:]
+    tx[p, 0] = both[16:]
+    tx[p, 1] = cross[at_piece, :]
     xr[row_slot] = both[:16]
     put_w = to_row_group(tx.at[p], tx.at[p], ss_w, rs_w.at[p])
     start_all(put_w, 16)
@@ -500,7 +504,7 @@
         sent_all(put_s, 16)
 
     all_landed(gfull, rs_h, 16, piece_at)
-    gram_all = gfull[:, 0].reshape(128, 128)
+    gram_all = gfull[...].reshape(128, 128)
     work[...] = gram_all
     loop(0, 128 // BLOCK, lambda k: cholesky_block(k, work, ut))
 
@@ -528,8 +532,7 @@
     inverse_t = dot(lower[...], upper[...], 0, 0, HIGH)
     work[...] = inverse_t
     root = ut[...]
-    turn = dot(gfull[:, 1].reshape(128, 128), root, 0, 0, HIGH)
-    rest = dot(dot(root, s1[:, 1].reshape(128, 128), 0, 0, HIGH), root, 1, 0, HIGH) - (turn + turn.T)
+    rest = dot(dot(root, s1[:, 1].reshape(128, 128), 0, 0, HIGH), root, 1, 0, HIGH)
 
     @pl.when(p >= 8)
     def _():
@@ -576,7 +579,8 @@
         put_z(0).wait_send()
 
     all_landed(tfull, rs_v, 16, piece_at)
-    wmat = tfull[...].reshape(128, 128) + rest
+    turn = dot(tfull[:, 1].reshape(128, 128), root, 0, 0, HIGH)
+    wmat = tfull[:, 0].reshape(128, 128) + (rest - (turn + turn.T))
     core = dot(dot(work[...], wmat, 0, 0, HIGH), work[...], 1, 0, HIGH)
     ch, cl = halves(dot3(ycols, core, 1, 1))
     for h in range(4):
@@ -594,39 +598,45 @@
 
 def step(psi, hpsi, counts, stored):
     vmem = pl.BlockSpec(memory_space=pltpu.VMEM)
+    far = pl.BlockSpec(memory_space=pltpu.HBM)
 
     def room(*dims):
         return pltpu.VMEM(dims, F32)
 
-    sems = [4, 32, 32, 32, 32, 4, 4, 32, 32, 16, 16, 16, 16, 16, 16, 16, 8, 16, 8, 16, 16, 32, 32, 32, 32, 16, 16, 16, 16, 16, 16]
+    sems = [6, 32, 32, 32, 32, 4, 4, 32, 32, 16, 16, 16, 16, 16, 16, 16, 8, 16, 8, 16, 16, 32, 32, 32, 32, 16, 16, 16, 16, 16, 16]
     return pl.pallas_call(
         step_kernel,
         name="step",
         out_shape=jax.ShapeDtypeStruct((1024, 128), F32),
-        in_specs=[pl.BlockSpec(memory_space=pltpu.HBM), vmem, pl.BlockSpec(memory_space=pltpu.SMEM), vmem],
+        in_specs=[far, far, pl.BlockSpec(memory_space=pltpu.SMEM), far],
         out_specs=vmem,
         scratch_shapes=[
-            pltpu.VMEM((4, 256, 2048), BF16), room(4, 4, 2, 2, 8, 16, 128),
+            pltpu.VMEM((256, 128), BF16), room(1024, 128), pltpu.VMEM((4, 256, 2048), BF16), room(4, 4, 2, 2, 8, 16, 128),
             room(4, 4, 2, 8, 16, 128), room(4, 8, 8, 8, 128), room(8, 4, 8, 8, 128),
             room(3, 8, 8, 8, 128), room(7, 4, 8, 8, 128), room(8, 8, 8, 128), room(4, 8, 8, 128),
             room(7, 8, 8, 128), room(3, 8, 8, 128), room(8, 2, 8, 128), room(7, 2, 8, 128),
             room(16, 128),
             room(32, 16, 128), room(16, 16, 128), room(32, 16, 256), room(32, 16, 128),
-            room(16, 16, 128), room(128, 128), room(128, 128), room(16, 2, 8, 128),
-            room(16, 2, 8, 128), room(8, 2, 16, 128), room(128, 128), room(8, 16, 256),
+            room(16, 16, 128), room(128, 128), room(128, 128), room(16, 8, 128),
+            room(16, 8, 128), room(8, 2, 16, 128), room(128, 128), room(8, 16, 256),
             room(2, 4, 2, 16, 256), room(16, 256), room(2, 16, 256), room(2, 16, 24, 128), room(16, 24, 128), room(16, 24, 128), room(128, 128),
             room(16, 24, 128), room(16, 128), room(32, 16, 128), room(16, 16, 128),
             room(128, 128), room(128, 128), room(128, 256), room(128, 256), room(128, 128),
-            room(128, 128), room(512, 128), room(256, 128), room(16, 8, 128), room(16, 8, 128),
+            room(128, 128), room(512, 128), room(256, 128), room(16, 2, 8, 128), room(16, 2, 8, 128),
         ] + [pltpu.SemaphoreType.DMA((k,)) for k in sems],
         compiler_params=pltpu.CompilerParams(
-            collective_id=1, has_side_effects=True, vmem_limit_bytes=62 << 20
+            collective_id=1, has_side_effects=True, vmem_limit_bytes=48 << 20
         ),
     )(psi, hpsi, counts, stored)
 
 
 def per_device(psi, hpsi, slab_counts, matrix):
-    return step(psi, hpsi, slab_counts, matrix.reshape(1024, 128)).reshape(matrix.shape)
+    def stay(array):
+        return pltpu.with_memory_space_constraint(array, pltpu.HBM)
+
+    return step(
+        stay(psi), stay(hpsi), slab_counts, stay(matrix.reshape(1024, 128))
+    ).reshape(matrix.shape)
 
 
 def solution(mesh):

time: 111 us -> 105 us (0.946); the launches traced: 110 us -> 105 us
  Pallas kernels: 107 us -> 104 us
  local copies, waits for them, and re-layouts: 2.19 us -> 0.8 us
    pallas_call x1, Pallas kernels: 107 us -> 104 us  [step(): pl.pallas_call(step_kernel, name='step', out_shape=jax.ShapeDtypeStruct((...]
    unnamed x1, local copies, waits for them, and re-layouts: 2.19 us -> 0.8 us
where the time goes in v5:
time: 105 us
  Pallas kernels  104 us (99%)
    pallas_call x1, Pallas kernels, step(): pl.pallas_call(step_kernel, name='step', out_shape=jax.ShapeDtypeStruct((...  104 us

profile of v5, /device:TPU:56, one launch (start us, length us, event | category | flops | bytes accessed | tf_op | source)
XLA Modules:
  0.0 105.0 jit_solution(7756867960174041553)
XLA Ops:
  0.7 103.5 %step.1 = f32[1024,128]{1,0:T(8,128)S(1)} custom-call(bf16[256,8192]{1,0:T(8,128)(2,1)} %psi.1, bf16[256,128]{1,0:T(8,128)(2,1)} %hpsi_far.1, s32[1]{0:T(128)S(6)} %copy.7.counts, f32[1024,128]{1,0:T(8,128)} %bitcast.3), custom_call_target="tpu_custom_call" | custom-call | tf_op jit(solution)/shard_map/step/pallas_call | solution.py:607
  104.2 0.8 copy.8

commit v6 on v5

--- a/solution.py
+++ b/solution.py
@@ -110,7 +110,7 @@
                 raw, rawt, xt, xo, xsum, tpart, xin, xown, xr, xc, work, ut, n, t, lower, upper, zr, zc, tx, tfull,
                 load, ss, rs, ss_b, rs_b, ss_p, rs_p, ss_r, rs_r, ss_c, rs_c, ss_g, rs_g, ss_h, rs_h,
                 ss_s, rs_s, ss_m, rs_m, ss_k, rs_k, ss_x, rs_x, ss_y, rs_y, ss_z, rs_z,
-                ss_w, rs_w, ss_v, rs_v):
+                ss_w, rs_w, ss_v, rs_v, ss_e, rs_e):
     p, q, zh, y, x, zl, c = position()
     z = zh * 4 + zl
     first = c == 0
@@ -323,10 +323,10 @@
     def landed(dst, sem):
         send(dst, dst, ss.at[0], sem, (p, q)).wait_recv()
 
-    put_r = to_col_group(own, srow.at[row_slot], ss_r, rs_r.at[row_slot])
+    put_r = to_col_group(own, srow.at[row_slot], ss_r, rs_r.at[0])
 
     def put_c(d):
-        return send(own, scol.at[q // 2], ss_c.at[d], rs_c.at[q // 2], ((p + d) % 16, home))
+        return send(own, scol.at[q // 2], ss_c.at[d], rs_c.at[0], ((p + d) % 16, home))
 
     start_all(put_r, 32)
     start_all(put_c, 16)
@@ -355,20 +355,16 @@
             landed(m1c.at[i], rs_m.at[i])
 
     def take_col(buffer, sem):
-        def take(j):
-            @pl.when((slot != p) | (2 * j + half != q))
-            def _():
-                landed(buffer.at[j], sem.at[j])
-
-        loop(0, 16, take)
+        @pl.when(at_home)
+        def _():
+            landed(buffer.at[pl.ds(0, 15)], sem.at[0])
+
+        @pl.when(jnp.logical_not(at_home))
+        def _():
+            landed(buffer, sem.at[0])
 
     def take_row(buffer, sem):
-        def take(d):
-            owner = (q + d) % 32
-            at_slot = 16 * (owner % 2) + owner // 2
-            landed(buffer.at[at_slot], sem.at[at_slot])
-
-        loop(1, 32, take)
+        landed(buffer.at[pl.ds(0, 31)], sem.at[0])
 
     take_row(srow, rs_r)
     zero = jnp.zeros((16, 128), F32)
@@ -382,9 +378,10 @@
     gram[...] = dot(low, low, 0, 0, HIGH)
     at_piece = pl.ds(pl.multiple_of(8 * piece_at, 8), 8)
     gx[p] = gram[at_piece, :]
-    put_g = to_row_group(gx.at[p], gx.at[p], ss_g, rs_g.at[p])
+    put_g = to_row_group(gx.at[p], gx.at[p], ss_g, rs_g.at[0])
     start_all(put_g, 16)
-    put_s = to_row_group(s1.at[from_panel], s1.at[from_panel], ss_s, rs_s.at[from_panel])
+    put_s = to_row_group(s1.at[from_panel, 0], s1.at[from_panel, 0], ss_s, rs_s.at[from_panel])
+    put_e = to_row_group(s1.at[from_panel, 1], s1.at[from_panel, 1], ss_e, rs_e.at[from_panel])
 
     lane = lax.broadcasted_iota(jnp.int32, (16, 128), 1)
     in_left = (lane < 16) & (q < 8)
@@ -422,7 +419,7 @@
 
     def put_x(d):
         to = (piece_at + d) % 16
-        return send(xsum.at[to], xin.at[piece_at], ss_x.at[d], rs_x.at[piece_at], (p, 2 * to + c))
+        return send(xsum.at[to], xin.at[piece_at], ss_x.at[d], rs_x.at[0], (p, 2 * to + c))
 
     start_all(put_x, 16)
     relay.wait_recv()
@@ -451,8 +448,8 @@
     def _():
         sent_all(put_k, 16)
 
-    def all_landed(buffer, sem, count, me):
-        loop(1, count, lambda d: landed(buffer.at[(me + d) % count], sem.at[(me + d) % count]))
+    def all_landed(buffer, sem, count):
+        landed(buffer.at[pl.ds(0, count - 1)], sem.at[0])
 
     def total_of(buffer, count):
         total = buffer[0]
@@ -463,28 +460,32 @@
     def put_piece(full, sem, got):
         def copy(d):
             to = (piece_at + d) % 16
-            return send(full.at[piece_at], full.at[piece_at], sem.at[d], got.at[piece_at], (p, 2 * to + c))
+            return send(full.at[piece_at], full.at[piece_at], sem.at[d], got.at[0], (p, 2 * to + c))
         return copy
 
-    all_landed(gx, rs_g, 16, p)
+    all_landed(gx, rs_g, 16)
     gfull[piece_at] = total_of(gx, 16)
     put_h = put_piece(gfull, ss_h, rs_h)
     start_all(put_h, 16)
 
-    all_landed(xin, rs_x, 16, piece_at)
+    all_landed(xin, rs_x, 16)
     xin[piece_at] = xsum[piece_at]
     both = total_of(xin, 16)
     xown[...] = both[:16]
     tx[p, 0] = both[16:]
     tx[p, 1] = cross[at_piece, :]
     xr[row_slot] = both[:16]
-    put_w = to_row_group(tx.at[p], tx.at[p], ss_w, rs_w.at[p])
+    put_w = to_row_group(tx.at[p], tx.at[p], ss_w, rs_w.at[0])
     start_all(put_w, 16)
-    put_y = to_col_group(xown, xr.at[row_slot], ss_y, rs_y.at[row_slot])
+    @pl.when(p >= 8)
+    def _():
+        start_all(put_e, 16)
+
+    put_y = to_col_group(xown, xr.at[row_slot], ss_y, rs_y.at[0])
     start_all(put_y, 32)
 
     def put_z(d):
-        return send(xown, xc.at[q // 2], ss_z.at[d], rs_z.at[q // 2], ((p + d) % 16, home))
+        return send(xown, xc.at[q // 2], ss_z.at[d], rs_z.at[0], ((p + d) % 16, home))
 
     start_all(put_z, 16)
 
@@ -503,7 +504,7 @@
     def _():
         sent_all(put_s, 16)
 
-    all_landed(gfull, rs_h, 16, piece_at)
+    all_landed(gfull, rs_h, 16)
     gram_all = gfull[...].reshape(128, 128)
     work[...] = gram_all
     loop(0, 128 // BLOCK, lambda k: cholesky_block(k, work, ut))
@@ -511,7 +512,7 @@
     def take_from_panel(i):
         @pl.when(i + 8 != p)
         def _():
-            landed(s1.at[i], rs_s.at[i])
+            landed(s1.at[i, 0], rs_s.at[i])
 
     loop(0, 8, take_from_panel)
     tops[...] = s1[:, 0].reshape(128, 128)
@@ -524,11 +525,17 @@
     t[:, :128] = normal.T
     t[:, 128:] = eye
     loop(0, 3, lambda k: inverse_block(k, n, t, lower, upper))
-    all_landed(tx, rs_w, 16, p)
+    all_landed(tx, rs_w, 16)
     tfull[piece_at] = total_of(tx, 16)
     put_v = put_piece(tfull, ss_v, rs_v)
     start_all(put_v, 16)
     loop(3, 128 // BLOCK, lambda k: inverse_block(k, n, t, lower, upper))
+    def take_corner(i):
+        @pl.when(i + 8 != p)
+        def _():
+            landed(s1.at[i, 1], rs_e.at[i])
+
+    loop(0, 8, take_corner)
     inverse_t = dot(lower[...], upper[...], 0, 0, HIGH)
     work[...] = inverse_t
     root = ut[...]
@@ -578,7 +585,7 @@
     def _():
         put_z(0).wait_send()
 
-    all_landed(tfull, rs_v, 16, piece_at)
+    all_landed(tfull, rs_v, 16)
     turn = dot(tfull[:, 1].reshape(128, 128), root, 0, 0, HIGH)
     wmat = tfull[:, 0].reshape(128, 128) + (rest - (turn + turn.T))
     core = dot(dot(work[...], wmat, 0, 0, HIGH), work[...], 1, 0, HIGH)
@@ -593,6 +600,11 @@
                 out[lines, :] = tile[:, 128 * k : 128 * k + 128]
 
     sent_all(put_v, 16)
+
+    @pl.when(p >= 8)
+    def _():
+        sent_all(put_e, 16)
+
     relay.wait_send()
 
 
@@ -603,7 +615,7 @@
     def room(*dims):
         return pltpu.VMEM(dims, F32)
 
-    sems = [6, 32, 32, 32, 32, 4, 4, 32, 32, 16, 16, 16, 16, 16, 16, 16, 8, 16, 8, 16, 16, 32, 32, 32, 32, 16, 16, 16, 16, 16, 16]
+    sems = [6, 32, 32, 32, 32, 4, 4, 32, 32, 16, 16, 16, 16, 16, 16, 16, 8, 16, 8, 16, 16, 32, 32, 32, 32, 16, 16, 16, 16, 16, 16, 16, 8]
     return pl.pallas_call(
         step_kernel,
         name="step",

time: 105 us -> 103 us (0.981); the launches traced: 105 us -> 101 us
  Pallas kernels: 104 us -> 99.6 us
    pallas_call x1, Pallas kernels: 104 us -> 99.6 us  [step(): pl.pallas_call(step_kernel, name='step', out_shape=jax.ShapeDtypeStruct((...]
where the time goes in v6:
time: 103 us; the launch traced here: 101 us
  Pallas kernels  99.6 us (97%)
    pallas_call x1, Pallas kernels, step(): pl.pallas_call(step_kernel, name='step', out_shape=jax.ShapeDtypeStruct((...  99.6 us

profile of v6, /device:TPU:56, one launch (start us, length us, event | category | flops | bytes accessed | tf_op | source)
XLA Modules:
  0.0 101.1 jit_solution(2531923468668194995)
XLA Ops:
  0.7 99.6 %step.1 = f32[1024,128]{1,0:T(8,128)S(1)} custom-call(bf16[256,8192]{1,0:T(8,128)(2,1)} %psi.1, bf16[256,128]{1,0:T(8,128)(2,1)} %hpsi_far.1, s32[1]{0:T(128)S(6)} %copy.7.counts, f32[1024,128]{1,0:T(8,128)} %bitcast.3), custom_call_target="tpu_custom_call" | custom-call | tf_op jit(solution)/shard_map/step/pallas_call | solution.py:619
  100.3 0.8 copy.8
